TPU v7x, 256 devices: a whole 4x4x8 slice. The times are simulated.
256 devices in a mesh: seq: 64 (over y, z, core), ch: 4 (over x).
Axes of the slice: x: 4, y: 4, z: 8, core: 2. Of those that a mesh axis runs over, the one named last changes fastest.
Arguments:
- inputs: bfloat16 [512, 512, 1024], P('seq', None, 'ch'), may hold values from -6 to 6
- cotangent: bfloat16 [512, 512, 1024], P(None, 'seq', 'ch'), may hold values from -6 to 6
- right_weight: bfloat16 [512, 512], replicated, may hold values from -0.25 to 0.25
- left_weight: bfloat16 [512, 512], replicated, may hold values from -0.25 to 0.25
- first_gate: bfloat16 [512, 1024], P(None, 'ch'), may hold values from -4 to 4
- second_gate: bfloat16 [512, 1024], P(None, 'ch'), may hold values from -4 to 4
Outputs:
- output: bfloat16 [512, 512, 1024], P(None, 'seq', 'ch')
- grad_inputs: bfloat16 [512, 512, 1024], P('seq', None, 'ch')
- grad_right: float32 [512, 512], P(('seq', 'ch'))
- grad_left: float32 [512, 512], P(('seq', 'ch'))
- grad_first_gate: float32 [512, 1024], P('seq', 'ch')
- grad_second_gate: float32 [512, 1024], P('seq', 'ch')
All inputs are finite; a program needn't handle non-finite values.
Results may differ from a plain program's by a relative error of at most 0.015.
Values may be sent and summed in bfloat16 or wider, within the bound.
A program may use at most 64 MiB of HBM per device.

v0:
```python
import jax
import jax.numpy as jnp
from jax import lax
from jax.sharding import PartitionSpec as P


def per_device(inputs, cotangent, right_weight, left_weight, first_gate, second_gate):
    section_one = jnp.einsum(
        "kj,ijd->ikd", right_weight, inputs, preferred_element_type=jnp.float32
    ).astype(jnp.bfloat16)
    gate_one = first_gate.astype(jnp.float32)[None, :, :]
    panels = (section_one.astype(jnp.float32) * gate_one).astype(jnp.bfloat16)
    received = lax.all_to_all(panels, "seq", split_axis=1, concat_axis=0, tiled=True)
    mixed = jnp.einsum("mi,ikd->mkd", left_weight, received, preferred_element_type=jnp.float32)
    logistic = jax.nn.sigmoid(mixed)
    activated = mixed * logistic
    gate_two = second_gate.astype(jnp.float32)[:, None, :]
    output = (activated * gate_two).astype(jnp.bfloat16)
    grad_out = cotangent.astype(jnp.float32)
    second_part = jnp.sum(grad_out * activated, axis=1)
    grad_mixed = (grad_out * gate_two * logistic * (1.0 + mixed * (1.0 - logistic))).astype(
        jnp.bfloat16
    )
    grad_left = lax.psum_scatter(
        jnp.einsum("mkd,ikd->mi", grad_mixed, received, preferred_element_type=jnp.float32),
        ("seq", "ch"),
        scatter_dimension=0,
        tiled=True,
    )
    grad_panels = jnp.einsum(
        "mi,mkd->ikd", left_weight, grad_mixed, preferred_element_type=jnp.float32
    ).astype(jnp.bfloat16)
    returned = lax.all_to_all(grad_panels, "seq", split_axis=0, concat_axis=1, tiled=True)
    returned32 = returned.astype(jnp.float32)
    first_part = jnp.sum(returned32 * section_one.astype(jnp.float32), axis=0)
    grad_section = (returned32 * gate_one).astype(jnp.bfloat16)
    grad_inputs = jnp.einsum(
        "kj,ikd->ijd", right_weight, grad_section, preferred_element_type=jnp.float32
    ).astype(jnp.bfloat16)
    grad_right = lax.psum_scatter(
        jnp.einsum("ikd,ijd->kj", grad_section, inputs, preferred_element_type=jnp.float32),
        ("seq", "ch"),
        scatter_dimension=0,
        tiled=True,
    )
    grad_first, grad_second = (
        lax.psum_scatter(first_part, "seq", scatter_dimension=0, tiled=True),
        lax.psum_scatter(second_part, "seq", scatter_dimension=0, tiled=True),
    )
    return (output, grad_inputs, grad_right, grad_left, grad_first, grad_second)


def solution(mesh):
    placed = (P("seq", None, "ch"), P(None, "seq", "ch"), P(), P(), P(None, "ch"), P(None, "ch"))
    return jax.shard_map(
        per_device,
        mesh=mesh,
        in_specs=placed,
        out_specs=(
            P(None, "seq", "ch"),
            P("seq", None, "ch"),
            P(("seq", "ch"), None),
            P(("seq", "ch"), None),
            P("seq", "ch"),
            P("seq", "ch"),
        ),
        check_vma=False,
    )
```

profile of v0, /device:TPU:24, one launch (start us, length us, event | category | flops | bytes accessed | tf_op | source)
XLA Modules:
  0.0 460.3 jit_solution(8371475585240869208)
XLA Ops:
  8.0 1.2 copy.59
  9.7 4.4 fusion.8
  14.0 4.5 copy.60
  18.5 12.4 %all-to-all-start = ((bf16[8,512,256]{2,0,1:T(8,128)(2,1)}), bf16[8,512,256]{2,0,1:T(8,128)(2,1)}, u32[]{:S(2)}, u32[]{:S(2)}) async-start(bf16[8,512,256]{2,0,1:T(8,128)(2,1)} %copy.60), calls=%async_computation | async-start | bytes 4194304 | tf_op jit(solution)/shard_map/all_to_all | solution.py:13
  31.1 4.3 copy.65
  35.4 44.4 %all-to-all-done = bf16[8,512,256]{2,0,1:T(8,128)(2,1)} async-done(((bf16[8,512,256]{2,0,1:T(8,128)(2,1)}), bf16[8,512,256]{2,0,1:T(8,128)(2,1)}, u32[]{:S(2)}, u32[]{:S(2)}) %all-to-all-start) | async-done | bytes 2097184 | tf_op jit(solution)/shard_map/all_to_all | solution.py:13
  79.8 2.4 copy.62
  82.2 5.5 %fusion.3 = (f32[512,256]{0,1:T(8,128)}, bf16[512,8,256]{0,2,1:T(8,128)(2,1)S(1)}, bf16[512,8,256]{0,2,1:T(8,128)(2,1)}) fusion(bf16[512,8,256]{0,2,1:T(8,128)(2,1)S(1)} %copy-done.3, f32[512,256]{0,1:T(8,128)S(1)} %copy.64, bf16[512,512]{1,0:T(8,128)(2,1)S(1)} %copy-done.6, bf16[512,8,256]{2,1,0:T(8,128)(2,1)S(1)} %bitcast.68), kind=kOutput, calls=%fused_computation.5 | convolution fusion | flops 1090387968 | bytes 9961472 | tf_op jit(solution)/shard_map/mi,ikd->mkd/dot_general | solution.py:14
  87.7 1.3 copy-done.7
  89.0 2.6 convert_bitcast_fusion.2
  91.6 4.5 copy.66
  96.1 8.3 %all-to-all-start.1 = ((bf16[512,8,256]{2,1,0:T(8,128)(2,1)}), bf16[512,8,256]{2,1,0:T(8,128)(2,1)}, u32[]{:S(2)}, u32[]{:S(2)}) async-start(bf16[512,8,256]{2,1,0:T(8,128)(2,1)} %copy.66), calls=%async_computation.1 | async-start | bytes 4194304 | tf_op jit(solution)/shard_map/all_to_all | solution.py:33
  104.5 4.5 fusion.14
  109.0 44.3 %all-to-all-done.1 = bf16[512,8,256]{2,1,0:T(8,128)(2,1)} async-done(((bf16[512,8,256]{2,1,0:T(8,128)(2,1)}), bf16[512,8,256]{2,1,0:T(8,128)(2,1)}, u32[]{:S(2)}, u32[]{:S(2)}) %all-to-all-start.1) | async-done | bytes 2097184 | tf_op jit(solution)/shard_map/all_to_all | solution.py:33
  153.2 3.9 copy_bitcast_fusion
  157.2 5.4 %copy.68 = f32[8,512,256]{1,2,0:T(8,128)} copy(f32[8,512,256]{2,1,0:T(8,128)} %copy_bitcast_fusion) | data formatting | bytes 8388608 | tf_op jit(solution)/shard_map/convert_element_type | solution.py:34
  162.6 4.6 convolution_bitcast_fusion
  169.2 3.6 fusion.9
  173.9 4.6 %copy.73 = bf16[512,8,256]{2,1,0:T(8,128)(2,1)} copy(bf16[512,8,256]{0,2,1:T(8,128)(2,1)} %get-tuple-element.34) | data formatting | bytes 4194304
  178.5 4.8 %convert_bitcast_fusion.1 = bf16[8,512,256]{1,2,0:T(8,128)(2,1)} fusion(f32[8,512,256]{1,2,0:T(8,128)} %copy.68, f32[512,256]{0,1:T(8,128)S(1)} %copy.59, bf16[512,512]{1,0:T(8,128)(2,1)S(1)} %copy-done.1), kind=kOutput, calls=%fused_computation.21 | convolution fusion | flops 1076887552 | bytes 7340032 | tf_op jit(solution)/shard_map/kj,ikd->ijd/dot_general | solution.py:37
  183.3 3.9 copy.74
  187.2 243.3 %all-reduce.5.cloned.1.call-done = (f32[512,512]{1,0:T(8,128)}, f32[512,512]{1,0:T(8,128)}) async-done(((f32[512,512]{1,0:T(8,128)}, f32[512,512]{1,0:T(8,128)}), (f32[512,512]{1,0:T(8,128)}, f32[512,512]{1,0:T(8,128)})) %all-reduce.5.cloned.1.call-update) | async-done | bytes 2097168
  430.5 1.3 constant_dynamic-slice_fusion
  431.9 21.0 %reduce-scatter.7.cloned.1.call-done = f32[8,256]{1,0:T(8,128)} async-done(((f32[512,256]{1,0:T(8,128)}), f32[8,256]{1,0:T(8,128)}) %reduce-scatter.7.cloned.1.call-update) | async-done | bytes 8208
  (25 shorter events, 3.7 us)
Async XLA Ops:
  8.0 1.7 copy-start
  18.5 12.4 %copy-start.5 = (bf16[512,256]{1,0:T(8,128)(2,1)S(1)}, bf16[512,256]{1,0:T(8,128)(2,1)}, u32[]{:S(2)}) copy-start(bf16[512,256]{1,0:T(8,128)(2,1)} %param.11) | copy-start | bytes 786436
  18.5 61.2 %all-to-all-start = ((bf16[8,512,256]{2,0,1:T(8,128)(2,1)}), bf16[8,512,256]{2,0,1:T(8,128)(2,1)}, u32[]{:S(2)}, u32[]{:S(2)}) async-start(bf16[8,512,256]{2,0,1:T(8,128)(2,1)} %copy.60), calls=%async_computation | async-start | bytes 4194304 | tf_op jit(solution)/shard_map/all_to_all | solution.py:13
  79.8 2.4 copy-start.3
  79.8 2.4 copy-start.6
  82.2 5.5 %copy-start.2 = (bf16[64,8,8,256]{3,2,1,0:T(8,128)(2,1)}, bf16[64,8,8,256]{3,2,1,0:T(8,128)(2,1)S(1)}, u32[]{:S(2)}) copy-start(bf16[64,8,8,256]{3,2,1,0:T(8,128)(2,1)S(1)} %copy.62) | copy-start | bytes 6291460
  87.7 1.3 copy-start.7
  96.1 57.1 %all-to-all-start.1 = ((bf16[512,8,256]{2,1,0:T(8,128)(2,1)}), bf16[512,8,256]{2,1,0:T(8,128)(2,1)}, u32[]{:S(2)}, u32[]{:S(2)}) async-start(bf16[512,8,256]{2,1,0:T(8,128)(2,1)} %copy.66), calls=%async_computation.1 | async-start | bytes 4194304 | tf_op jit(solution)/shard_map/all_to_all | solution.py:33
  104.4 326.1 %all-reduce.5.cloned.1.call-start = ((), (), s32[]{:S(2)}) async-start(), calls=%async_computation.6 | async-start | bytes 4194304
  167.1 1.0 copy-start.4
  167.1 264.8 %reduce-scatter.9.cloned.1.call-start = ((), (), s32[]{:S(2)}) async-start(), calls=%async_computation.5 | async-start | bytes 532480
  169.2 283.7 %reduce-scatter.7.cloned.1.call-start = ((), (), s32[]{:S(2)}) async-start(), calls=%async_computation.4 | async-start | bytes 532480
  173.9 4.6 %copy-start.1 = (bf16[512,512]{1,0:T(8,128)(2,1)S(1)}, bf16[512,512]{1,0:T(8,128)(2,1)}, u32[]{:S(2)}) copy-start(bf16[512,512]{1,0:T(8,128)(2,1)} %param.8) | copy-start | bytes 1572868
Sparse Core Ops, SparseCore 0:
  167.3 263.2 all-reduce.4
Sparse Core Ops, SparseCore 1:
  172.2 137.9 reduce-scatter.8
  314.5 138.3 reduce-scatter.6
where the time goes:
time: 462 us; the launch traced here: 460 us
  waiting for transfers between devices  353 us (76%)
  local copies, waits for them, and re-layouts  36.8 us (8%)
  matrix products  26.3 us (6%)
  starting transfers between devices  21 us (5%)
  between operations  15.6 us (3%)
  other arithmetic  7.54 us (2%)
    unnamed x6, waiting for transfers between devices  264 us
    all_to_all x1, waiting for transfers between devices, per_device(): lax.all_to_all(panels, 'seq', split_axis=1, concat_axis=0, tiled=True)  44.4 us
    all_to_all x1, waiting for transfers between devices, per_device(): lax.all_to_all(grad_panels, 'seq', split_axis=0, concat_axis=1, tiled=True)  44.3 us
    unnamed x22, local copies, waits for them, and re-layouts  18.7 us
    all_to_all x1, starting transfers between devices, per_device(): lax.all_to_all(panels, 'seq', split_axis=1, concat_axis=0, tiled=True)  12.4 us
  transfers between devices with their start and end apart: 5, of which 4 were waited for; matrix products, arithmetic and copies ran while one was open for 6% of the time, Pallas kernels for 0%

commit v1 on v0

--- a/solution.py
+++ b/solution.py
@@ -21,12 +21,13 @@
     grad_mixed = (grad_out * gate_two * logistic * (1.0 + mixed * (1.0 - logistic))).astype(
         jnp.bfloat16
     )
-    grad_left = lax.psum_scatter(
-        jnp.einsum("mkd,ikd->mi", grad_mixed, received, preferred_element_type=jnp.float32),
-        ("seq", "ch"),
-        scatter_dimension=0,
-        tiled=True,
+    left_part = jnp.einsum("mkd,ikd->mi", grad_mixed, received, preferred_element_type=jnp.float32)
+    early = lax.psum_scatter(
+        jnp.concatenate([left_part, second_part], axis=1), "seq", scatter_dimension=0, tiled=True
     )
+    order = left_part.shape[1]
+    grad_left = lax.psum_scatter(early[:, :order], "ch", scatter_dimension=0, tiled=True)
+    grad_second = early[:, order:]
     grad_panels = jnp.einsum(
         "mi,mkd->ikd", left_weight, grad_mixed, preferred_element_type=jnp.float32
     ).astype(jnp.bfloat16)
@@ -37,16 +38,13 @@
     grad_inputs = jnp.einsum(
         "kj,ikd->ijd", right_weight, grad_section, preferred_element_type=jnp.float32
     ).astype(jnp.bfloat16)
-    grad_right = lax.psum_scatter(
-        jnp.einsum("ikd,ijd->kj", grad_section, inputs, preferred_element_type=jnp.float32),
-        ("seq", "ch"),
-        scatter_dimension=0,
-        tiled=True,
+    right_part = jnp.einsum("ikd,ijd->kj", grad_section, inputs, preferred_element_type=jnp.float32)
+    late = lax.psum_scatter(
+        jnp.concatenate([right_part, first_part], axis=1), "seq", scatter_dimension=0, tiled=True
     )
-    grad_first, grad_second = (
-        lax.psum_scatter(first_part, "seq", scatter_dimension=0, tiled=True),
-        lax.psum_scatter(second_part, "seq", scatter_dimension=0, tiled=True),
-    )
+    order = right_part.shape[1]
+    grad_right = lax.psum_scatter(late[:, :order], "ch", scatter_dimension=0, tiled=True)
+    grad_first = late[:, order:]
     return (output, grad_inputs, grad_right, grad_left, grad_first, grad_second)
 
 

time: 462 us -> 431 us (0.933)
  waiting for transfers between devices: 353 us -> 293 us
  blocking collectives: 0 us -> 22.5 us
  local copies, waits for them, and re-layouts: 36.8 us -> 45.7 us
    unnamed x6 -> x4, waiting for transfers between devices: 264 us -> 208 us
    unnamed x0 -> x1, blocking collectives: none -> 22.5 us
    unnamed x22 -> x31, local copies, waits for them, and re-layouts: 18.7 us -> 23.5 us
  transfers between devices with their start and end apart: 5 -> 4, of which waited for: 4 -> 4; matrix products, arithmetic and copies ran while one was open for 6% -> 11% of each run, Pallas kernels for 0% -> 0%
where the time goes in v1:
time: 431 us; the launch traced here: 429 us
  waiting for transfers between devices  293 us (68%)
  local copies, waits for them, and re-layouts  45.7 us (11%)
  blocking collectives  22.5 us (5%)
  matrix products  22 us (5%)
  starting transfers between devices  21 us (5%)
  between operations  14.9 us (3%)
  other arithmetic  10.4 us (2%)
    unnamed x4, waiting for transfers between devices  208 us
    all_to_all x1, waiting for transfers between devices, per_device(): lax.all_to_all(panels, 'seq', split_axis=1, concat_axis=0, tiled=True)  44.4 us
    all_to_all x1, waiting for transfers between devices, per_device(): lax.all_to_all(grad_panels, 'seq', split_axis=0, concat_axis=1, tiled=True)  40.5 us
    unnamed x31, local copies, waits for them, and re-layouts  23.5 us
    unnamed x1, blocking collectives  22.5 us
    all_to_all x1, starting transfers between devices, per_device(): lax.all_to_all(panels, 'seq', split_axis=1, concat_axis=0, tiled=True)  12.4 us
  transfers between devices with their start and end apart: 4, of which 4 were waited for; matrix products, arithmetic and copies ran while one was open for 11% of the time, Pallas kernels for 0%

profile of v1, /device:TPU:24, one launch (start us, length us, event | category | flops | bytes accessed | tf_op | source)
XLA Modules:
  0.0 429.4 jit_solution(6826681556601042458)
XLA Ops:
  8.8 4.4 %fusion.8 = (bf16[8,512,256]{1,2,0:T(8,128)(2,1)}, bf16[8,256,512]{2,1,0:T(8,128)(2,1)}) fusion(f32[512,256]{0,1:T(8,128)S(1)} %copy.48, bf16[8,512,256]{2,1,0:T(8,128)(2,1)S(1)} %copy-done, bf16[512,512]{1,0:T(8,128)(2,1)} %param.8), kind=kOutput, calls=%fused_computation.16 | convolution fusion | flops 1077936128 | bytes 7340032 | tf_op jit(solution)/shard_map/kj,ijd->ikd/dot_general | solution.py:8
  13.2 4.5 %copy.49 = bf16[8,512,256]{2,0,1:T(8,128)(2,1)} copy(bf16[8,512,256]{1,2,0:T(8,128)(2,1)} %get-tuple-element.29) | data formatting | bytes 4194304 | tf_op jit(solution)/shard_map/convert_element_type | solution.py:12
  17.7 12.4 %all-to-all-start = ((bf16[8,512,256]{2,0,1:T(8,128)(2,1)}), bf16[8,512,256]{2,0,1:T(8,128)(2,1)}, u32[]{:S(2)}, u32[]{:S(2)}) async-start(bf16[8,512,256]{2,0,1:T(8,128)(2,1)} %copy.49), calls=%async_computation | async-start | bytes 4194304 | tf_op jit(solution)/shard_map/all_to_all | solution.py:13
  30.3 4.3 copy.54
  34.5 44.4 %all-to-all-done = bf16[8,512,256]{2,0,1:T(8,128)(2,1)} async-done(((bf16[8,512,256]{2,0,1:T(8,128)(2,1)}), bf16[8,512,256]{2,0,1:T(8,128)(2,1)}, u32[]{:S(2)}, u32[]{:S(2)}) %all-to-all-start) | async-done | bytes 2097184 | tf_op jit(solution)/shard_map/all_to_all | solution.py:13
  78.9 2.4 copy.51
  81.4 5.5 %fusion.3 = (f32[512,256]{0,1:T(8,128)}, bf16[512,8,256]{0,2,1:T(8,128)(2,1)S(1)}, bf16[512,8,256]{0,2,1:T(8,128)(2,1)}) fusion(bf16[512,8,256]{0,2,1:T(8,128)(2,1)S(1)} %copy-done.4, f32[512,256]{0,1:T(8,128)S(1)} %copy.53, bf16[512,512]{1,0:T(8,128)(2,1)S(1)} %copy-done.7, bf16[512,8,256]{2,1,0:T(8,128)(2,1)S(1)} %bitcast.73), kind=kOutput, calls=%fused_computation.5 | convolution fusion | flops 1090387968 | bytes 9961472 | tf_op jit(solution)/shard_map/mi,ikd->mkd/dot_general | solution.py:14
  88.3 2.6 convert_bitcast_fusion.2
  90.9 4.5 %copy.55 = bf16[512,8,256]{2,1,0:T(8,128)(2,1)} copy(bf16[512,8,256]{0,2,1:T(8,128)(2,1)} %convert_bitcast_fusion.2) | data formatting | bytes 4194304 | tf_op jit(solution)/shard_map/convert_element_type | solution.py:33
  95.4 8.3 %all-to-all-start.1 = ((bf16[512,8,256]{2,1,0:T(8,128)(2,1)}), bf16[512,8,256]{2,1,0:T(8,128)(2,1)}, u32[]{:S(2)}, u32[]{:S(2)}) async-start(bf16[512,8,256]{2,1,0:T(8,128)(2,1)} %copy.55), calls=%async_computation.1 | async-start | bytes 4194304 | tf_op jit(solution)/shard_map/all_to_all | solution.py:34
  103.7 3.5 fusion.14
  107.3 1.4 pad_maximum_fusion.1
  108.6 3.1 copy.76
  112.0 40.5 %all-to-all-done.1 = bf16[512,8,256]{2,1,0:T(8,128)(2,1)} async-done(((bf16[512,8,256]{2,1,0:T(8,128)(2,1)}), bf16[512,8,256]{2,1,0:T(8,128)(2,1)}, u32[]{:S(2)}, u32[]{:S(2)}) %all-to-all-start.1) | async-done | bytes 2097184 | tf_op jit(solution)/shard_map/all_to_all | solution.py:34
  152.5 4.0 copy_bitcast_fusion
  156.5 5.4 %copy.57 = f32[8,512,256]{1,2,0:T(8,128)} copy(f32[8,512,256]{2,1,0:T(8,128)} %copy_bitcast_fusion) | data formatting | bytes 8388608 | tf_op jit(solution)/shard_map/convert_element_type | solution.py:35
  161.9 3.8 fusion.9
  168.5 3.1 copy.72
  172.9 4.6 %copy.62 = bf16[512,8,256]{2,1,0:T(8,128)(2,1)} copy(bf16[512,8,256]{0,2,1:T(8,128)(2,1)} %get-tuple-element.28) | data formatting | bytes 4194304
  177.4 75.5 %reduce-scatter.11.cloned.1.call-done = f32[8,768]{1,0:T(8,128)} async-done(((f32[512,768]{1,0:T(8,128)}), f32[8,768]{1,0:T(8,128)}) %reduce-scatter.11.cloned.1.call-update) | async-done | bytes 24592
  255.1 4.8 %convert_bitcast_fusion.1 = bf16[8,512,256]{1,2,0:T(8,128)(2,1)} fusion(f32[8,512,256]{1,2,0:T(8,128)} %copy.57, f32[512,256]{0,1:T(8,128)S(1)} %copy.48, bf16[512,512]{1,0:T(8,128)(2,1)S(1)} %copy-done.2), kind=kOutput, calls=%fused_computation.21 | convolution fusion | flops 1076887552 | bytes 7340032 | tf_op jit(solution)/shard_map/kj,ikd->ijd/dot_general | solution.py:38
  259.9 3.9 copy.63
  263.8 132.5 %reduce-scatter.9.cloned.1.call-done = f32[8,768]{1,0:T(8,128)} async-done(((f32[512,768]{1,0:T(8,128)}), f32[8,768]{1,0:T(8,128)}) %reduce-scatter.9.cloned.1.call-update) | async-done | bytes 24592
  397.1 22.5 %all-reduce.2 = (f32[8,512]{0,1:T(8,128)S(1)}, f32[8,512]{0,1:T(8,128)S(1)}) all-reduce(f32[8,512]{0,1:T(8,128)S(1)} %copy.80, f32[8,512]{0,1:T(8,128)S(1)} %copy.81), channel_id=3, replica_groups=mesh['seq'=64,'ch'=4] {'ch'}, use_global_device_ids=true, to_apply=%region_2.0.clone | all-reduce | flops 8192 | bytes 65536
  (38 shorter events, 12.8 us)
Async XLA Ops:
  7.2 1.7 copy-start
  17.7 12.4 %copy-start.6 = (bf16[512,256]{1,0:T(8,128)(2,1)S(1)}, bf16[512,256]{1,0:T(8,128)(2,1)}, u32[]{:S(2)}) copy-start(bf16[512,256]{1,0:T(8,128)(2,1)} %param.11) | copy-start | bytes 786436
  17.7 61.2 %all-to-all-start = ((bf16[8,512,256]{2,0,1:T(8,128)(2,1)}), bf16[8,512,256]{2,0,1:T(8,128)(2,1)}, u32[]{:S(2)}, u32[]{:S(2)}) async-start(bf16[8,512,256]{2,0,1:T(8,128)(2,1)} %copy.49), calls=%async_computation | async-start | bytes 4194304 | tf_op jit(solution)/shard_map/all_to_all | solution.py:13
  78.9 2.4 copy-start.4
  78.9 2.4 copy-start.7
  81.4 5.5 %copy-start.3 = (bf16[64,8,8,256]{3,2,1,0:T(8,128)(2,1)}, bf16[64,8,8,256]{3,2,1,0:T(8,128)(2,1)S(1)}, u32[]{:S(2)}) copy-start(bf16[64,8,8,256]{3,2,1,0:T(8,128)(2,1)S(1)} %copy.51) | copy-start | bytes 6291460
  86.9 1.4 copy-start.9
  95.4 57.1 %all-to-all-start.1 = ((bf16[512,8,256]{2,1,0:T(8,128)(2,1)}), bf16[512,8,256]{2,1,0:T(8,128)(2,1)}, u32[]{:S(2)}, u32[]{:S(2)}) async-start(bf16[512,8,256]{2,1,0:T(8,128)(2,1)} %copy.55), calls=%async_computation.1 | async-start | bytes 4194304 | tf_op jit(solution)/shard_map/all_to_all | solution.py:34
  103.7 3.6 copy-start.5
  103.7 149.3 %reduce-scatter.11.cloned.1.call-start = ((), (), s32[]{:S(2)}) async-start(), calls=%async_computation.5 | async-start | bytes 1597440
  111.7 284.6 %reduce-scatter.9.cloned.1.call-start = ((), (), s32[]{:S(2)}) async-start(), calls=%async_computation.4 | async-start | bytes 1597440
  161.9 4.1 copy-start.1
  168.5 3.1 copy-start.8
  172.9 82.3 %copy-start.2 = (bf16[512,512]{1,0:T(8,128)(2,1)S(1)}, bf16[512,512]{1,0:T(8,128)(2,1)}, u32[]{:S(2)}) copy-start(bf16[512,512]{1,0:T(8,128)(2,1)} %param.8) | copy-start | bytes 1572868
Sparse Core Ops, SparseCore 0:
  111.9 141.0 reduce-scatter.10
  257.0 139.2 reduce-scatter.8

commit v2 on v1

v2 whole, which is shorter than its diff:
```python
import functools

import jax
import jax.numpy as jnp
from jax import lax
from jax.experimental import pallas as pl
from jax.experimental.pallas import tpu as pltpu
from jax.sharding import PartitionSpec as P

MESH = pl.DeviceIdType.MESH
F32 = jnp.float32
BF16 = jnp.bfloat16
LANES = 128
ROWS = 64


def dot(a, b, contract):
    return lax.dot_general(a, b, ((contract[:1], contract[1:]), ((), ())), preferred_element_type=F32)


def fused(
    seqs, chs, grid,
    x_hbm, ct_hbm, right_hbm, left_hbm, gate1_hbm, gate2_hbm,
    out_hbm, gi_hbm, gr_out, gl_out, gf_out, gs_out,
    xv, ctv, right, left, gate1, gate2, ov, giv,
    right_t, left_t, s1, flat, flat_out, prod, pair, grad_pair, gl, gr, gfirst, gsecond,
    fsend, frecv, bsend, brecv,
    csend, crecv, cgsend, cgrecv, half, xsend, xrecv, quarter, zsend, zrecv, zgsend, zgrecv,
    in_sem, out_sem, fs_sem, fr_sem, bs_sem, br_sem, r_sem,
):
    s, ch = lax.axis_index("seq"), lax.axis_index("ch")
    core = s % 2
    own = s // 2
    pairs = seqs // 2
    blocks = grid // ROWS

    barrier = pltpu.get_barrier_semaphore()

    def greet(t, _):
        pl.semaphore_signal(barrier, inc=1, device_id=((s + t) % seqs, ch), device_id_type=MESH)
        return 0

    def greet_ch(t, _):
        pl.semaphore_signal(barrier, inc=1, device_id=(s, (ch + t) % chs), device_id_type=MESH)
        return 0

    loads = [
        pltpu.make_async_copy(src, dst, in_sem.at[n])
        for n, (src, dst) in enumerate(
            ((x_hbm, xv), (right_hbm, right), (gate1_hbm, gate1), (ct_hbm, ctv), (left_hbm, left), (gate2_hbm, gate2))
        )
    ]
    for load in loads:
        load.start()
    lax.fori_loop(1, seqs, greet, 0)
    lax.fori_loop(1, chs, greet_ch, 0)
    for load in loads[:3]:
        load.wait()

    def half_of(h):
        return slice(h * LANES, (h + 1) * LANES)

    def x_pair(h, ip):
        return jnp.concatenate([xv[2 * ip, :, half_of(h)], xv[2 * ip + 1, :, half_of(h)]], axis=1)

    def exchange(h, src, dst, send_sem, recv_sem):
        pltpu.make_async_copy(src.at[h, s], dst.at[h, s], recv_sem.at[h]).start()

        def send(t, _):
            d = (s + t) % seqs
            pltpu.make_async_remote_copy(
                src_ref=src.at[h, d], dst_ref=dst.at[h, s], send_sem=send_sem.at[h], recv_sem=recv_sem.at[h],
                device_id=(d, ch), device_id_type=MESH,
            ).start()
            return 0

        lax.fori_loop(1, seqs, send, 0)

    def arrived(dst, sem):
        pltpu.make_async_copy(dst, dst, sem).wait()

    def first_stage(h):
        def per_pair(ip, _):
            prod[...] = dot(right[...], x_pair(h, ip), (1, 0))

            def rows(b, _):
                r = pl.ds(pl.multiple_of(b * ROWS, ROWS), ROWS)
                gate = gate1[r, half_of(h)].astype(F32)
                for e in range(2):
                    section = prod[r, half_of(e)].astype(BF16)
                    s1[2 * ip + e, h, r, :] = section
                    flat[pl.ds(b * (ROWS * 8) + 2 * ip + e, ROWS, stride=8), :] = section.astype(F32) * gate
                return 0

            lax.fori_loop(0, blocks, rows, 0)
            return 0

        lax.fori_loop(0, 4, per_pair, 0)

        def pack(d, _):
            rows = flat[pl.ds(pl.multiple_of(d * 64, 64), 64), :]
            fsend[h, d] = rows.reshape(8, 8, LANES).astype(BF16)
            return 0

        lax.fori_loop(0, seqs, pack, 0, unroll=4)

    def middle(h):
        def unpack(b, _):
            m = pl.ds(pl.multiple_of(b * 8, 8), 8)
            flat[pl.ds(pl.multiple_of(b * 64, 64), 64), :] = ctv[m, :, half_of(h)].astype(F32).reshape(64, LANES)
            return 0

        lax.fori_loop(0, grid // 8, unpack, 0, unroll=4)
        gsecond[:, half_of(h)] = jnp.zeros((grid, LANES), F32)
        arrived(frecv.at[h], fr_sem.at[h])

        def per_pair(kp, _):
            pair[...] = jnp.concatenate(
                [frecv[h, :, 2 * kp + e].astype(F32).reshape(grid, LANES).astype(BF16) for e in range(2)], axis=1
            )
            prod[...] = dot(left[...], pair[...], (1, 0))

            def rows(b, _):
                r = pl.ds(pl.multiple_of(b * ROWS, ROWS), ROWS)
                gate = gate2[r, half_of(h)].astype(F32)
                total = gsecond[r, half_of(h)]
                for e in range(2):
                    at = pl.ds(b * (ROWS * 8) + 2 * kp + e, ROWS, stride=8)
                    mixed = prod[r, half_of(e)]
                    grad_out = flat[at, :]
                    logistic = 1.0 / (1.0 + jnp.exp(-mixed))
                    activated = mixed * logistic
                    flat_out[at, :] = activated * gate
                    total = total + grad_out * activated
                    grad_mixed = grad_out * gate * logistic * (1.0 + mixed * (1.0 - logistic))
                    grad_pair[r, half_of(e)] = grad_mixed.astype(BF16)
                gsecond[r, half_of(h)] = total
                return 0

            lax.fori_loop(0, blocks, rows, 0)
            gl[...] += dot(grad_pair[...], pair[...], (1, 1))
            prod[...] = dot(left_t[...], grad_pair[...], (1, 0))
            for e in range(2):
                bsend[h, :, 2 * kp + e] = prod[:, half_of(e)].reshape(seqs, 8, LANES).astype(BF16)
            return 0

        lax.fori_loop(0, 4, per_pair, 0)

    def write_out(h):
        def pack(b, _):
            m = pl.ds(pl.multiple_of(b * 8, 8), 8)
            rows = flat_out[pl.ds(pl.multiple_of(b * 64, 64), 64), :]
            ov[m, :, half_of(h)] = rows.reshape(8, 8, LANES).astype(BF16)
            return 0

        lax.fori_loop(0, grid // 8, pack, 0, unroll=4)

    def last_stage(h):
        gfirst[:, half_of(h)] = jnp.zeros((grid, LANES), F32)
        arrived(brecv.at[h], br_sem.at[h])

        def unpack(b, _):
            rows = brecv[h, b].astype(F32).reshape(64, LANES)
            flat[pl.ds(pl.multiple_of(b * 64, 64), 64), :] = rows
            return 0

        lax.fori_loop(0, seqs, unpack, 0, unroll=4)

        def per_pair(ip, _):
            def rows(b, _):
                r = pl.ds(pl.multiple_of(b * ROWS, ROWS), ROWS)
                gate = gate1[r, half_of(h)].astype(F32)
                total = gfirst[r, half_of(h)]
                for e in range(2):
                    grad = flat[pl.ds(b * (ROWS * 8) + 2 * ip + e, ROWS, stride=8), :]
                    total = total + grad * s1[2 * ip + e, h, r, :].astype(F32)
                    grad_pair[r, half_of(e)] = (grad * gate).astype(BF16)
                gfirst[r, half_of(h)] = total
                return 0

            lax.fori_loop(0, blocks, rows, 0)
            gr[...] += dot(grad_pair[...], x_pair(h, ip), (1, 1))
            prod[...] = dot(right_t[...], grad_pair[...], (1, 0))
            for e in range(2):
                giv[2 * ip + e, :, half_of(h)] = prod[:, half_of(e)].astype(BF16)
            return 0

        lax.fori_loop(0, 4, per_pair, 0)

    def reduce(n, matrix, gates, matrix_out, gates_out):
        sems = r_sem.at[n]

        def give(p, _):
            r = pl.ds(pl.multiple_of(p * 16 + (1 - core) * 8, 8), 8)
            csend[n, p] = matrix[r, :].astype(BF16)
            cgsend[n, p] = gates[r, :].astype(BF16)
            return 0

        lax.fori_loop(0, pairs, give, 0, unroll=2)
        copies = [
            pltpu.make_async_remote_copy(
                src_ref=src.at[n], dst_ref=dst.at[n], send_sem=sems.at[2 * q], recv_sem=sems.at[2 * q + 1],
                device_id=(s + 1 - 2 * core, ch), device_id_type=MESH,
            )
            for q, (src, dst) in enumerate(((csend, crecv), (cgsend, cgrecv)))
        ]
        for copy in copies:
            copy.start()
        for copy in copies:
            copy.wait()

        def take(p, _):
            r = pl.ds(pl.multiple_of(p * 16 + core * 8, 8), 8)
            total = matrix[r, :] + crecv[n, p].astype(F32)
            for c in range(4):
                half[c, pl.ds(pl.multiple_of(p * 8, 8), 8), :] = total[:, c * LANES : (c + 1) * LANES]
            zgsend[n, p] = (gates[r, :] + cgrecv[n, p].astype(F32)).astype(BF16)
            return 0

        lax.fori_loop(0, pairs, take, 0, unroll=2)
        for a in range(chs):
            for b in range(2):
                for c in range(4):
                    lanes = slice(c * LANES, (c + 1) * LANES)
                    xsend[n, a, b, :, lanes] = half[c, pl.ds(2 * a + b, pairs, stride=8), :].astype(BF16)
        pltpu.make_async_copy(xsend.at[n, ch], xrecv.at[n, ch], sems.at[5]).start()

        def send_ch(t, _):
            d = (ch + t) % chs
            pltpu.make_async_remote_copy(
                src_ref=xsend.at[n, d], dst_ref=xrecv.at[n, ch], send_sem=sems.at[4], recv_sem=sems.at[5],
                device_id=(s, d), device_id_type=MESH,
            ).start()
            return 0

        lax.fori_loop(1, chs, send_ch, 0)
        pltpu.make_async_copy(zgsend.at[n, own], zgrecv.at[n, own], sems.at[9]).start()

        def send_gates(t, _):
            d = (own + t) % pairs
            pltpu.make_async_remote_copy(
                src_ref=zgsend.at[n, d], dst_ref=zgrecv.at[n, own], send_sem=sems.at[8], recv_sem=sems.at[9],
                device_id=(2 * d + core, ch), device_id_type=MESH,
            ).start()
            return 0

        lax.fori_loop(1, pairs, send_gates, 0)
        arrived(xrecv.at[n], sems.at[5])
        total = xrecv[n, 0].astype(F32)
        for a in range(1, chs):
            total = total + xrecv[n, a].astype(F32)
        for c in range(4):
            quarter[c] = total.reshape(2 * pairs, grid)[:, c * LANES : (c + 1) * LANES]
        for p in range(pairs):
            for c in range(4):
                lanes = slice(c * LANES, (c + 1) * LANES)
                zsend[n, p, :, lanes] = quarter[c, pl.ds(p, 2, stride=pairs), :].astype(BF16)
        pltpu.make_async_copy(zsend.at[n, own], zrecv.at[n, own], sems.at[7]).start()

        def send_rows(t, _):
            d = (own + t) % pairs
            pltpu.make_async_remote_copy(
                src_ref=zsend.at[n, d], dst_ref=zrecv.at[n, own], send_sem=sems.at[6], recv_sem=sems.at[7],
                device_id=(2 * d + core, ch), device_id_type=MESH,
            ).start()
            return 0

        lax.fori_loop(1, pairs, send_rows, 0)
        arrived(zgrecv.at[n], sems.at[9])
        gates_out[...] = jnp.sum(zgrecv[n].astype(F32), axis=0)
        arrived(zrecv.at[n], sems.at[7])
        matrix_out[...] = jnp.sum(zrecv[n].astype(F32), axis=0)
        arrived(xsend.at[n, pl.ds(0, chs - 1)], sems.at[4])
        arrived(zsend.at[n, pl.ds(0, pairs - 1)], sems.at[6])
        arrived(zgsend.at[n, pl.ds(0, pairs - 1)], sems.at[8])

    first_stage(0)
    pl.semaphore_wait(barrier, seqs + chs - 2)
    exchange(0, fsend, frecv, fs_sem, fr_sem)
    first_stage(1)
    exchange(1, fsend, frecv, fs_sem, fr_sem)
    for load in loads[3:]:
        load.wait()
    right_t[...] = right[...].T
    left_t[...] = left[...].T
    gl[...] = jnp.zeros(gl.shape, F32)
    gr[...] = jnp.zeros(gr.shape, F32)
    stores = []
    for h in range(2):
        middle(h)
        exchange(h, bsend, brecv, bs_sem, br_sem)
        write_out(h)
    store = pltpu.make_async_copy(ov, out_hbm, out_sem.at[0])
    store.start()
    stores.append(store)
    reduce(0, gl, gsecond, gl_out, gs_out)
    for h in range(2):
        last_stage(h)
    store = pltpu.make_async_copy(giv, gi_hbm, out_sem.at[1])
    store.start()
    stores.append(store)
    reduce(1, gr, gfirst, gr_out, gf_out)
    for store in stores:
        store.wait()
    for h in range(2):
        arrived(fsend.at[h, pl.ds(0, seqs - 1)], fs_sem.at[h])
        arrived(bsend.at[h, pl.ds(0, seqs - 1)], bs_sem.at[h])


def per_device(seqs, chs, inputs, cotangent, right_weight, left_weight, first_gate, second_gate):
    rows, grid, width = inputs.shape
    hbm = pl.BlockSpec(memory_space=pl.ANY)
    vmem = pl.BlockSpec(memory_space=pltpu.VMEM)
    pairs = seqs // 2
    block = (2, seqs, 8, 8, LANES)

    def v(shape, dtype=BF16):
        return pltpu.VMEM(shape, dtype)

    dma = pltpu.SemaphoreType.DMA
    out, gi, gr, gl, gf, gs = pl.pallas_call(
        functools.partial(fused, seqs, chs, grid),
        out_shape=(
            jax.ShapeDtypeStruct(cotangent.shape, BF16),
            jax.ShapeDtypeStruct(inputs.shape, BF16),
            jax.ShapeDtypeStruct((2, grid), F32),
            jax.ShapeDtypeStruct((2, grid), F32),
            jax.ShapeDtypeStruct((8, width), F32),
            jax.ShapeDtypeStruct((8, width), F32),
        ),
        in_specs=[hbm] * 6,
        out_specs=(hbm, hbm, vmem, vmem, vmem, vmem),
        scratch_shapes=[
            v(inputs.shape), v(cotangent.shape), v((grid, grid)), v((grid, grid)), v((grid, width)), v((grid, width)),
            v(cotangent.shape), v(inputs.shape),
            v((grid, grid)), v((grid, grid)), v((8, 2, grid, LANES)), v((grid * 8, LANES), F32), v((grid * 8, LANES), F32),
            v((grid, 2 * LANES), F32), v((grid, 2 * LANES)), v((grid, 2 * LANES)),
            v((grid, grid), F32), v((grid, grid), F32), v((grid, width), F32), v((grid, width), F32),
            v(block), v(block), v(block), v(block),
            v((2, pairs, 8, grid)), v((2, pairs, 8, grid)), v((2, pairs, 8, width)), v((2, pairs, 8, width)),
            v((4, pairs * 8, LANES), F32), v((2, chs, 2, pairs, grid)), v((2, chs, 2, pairs, grid)),
            v((4, 2 * pairs, LANES), F32), v((2, pairs, 2, grid)), v((2, pairs, 2, grid)),
            v((2, pairs, 8, width)), v((2, pairs, 8, width)),
            dma((6,)), dma((2,)), dma((2,)), dma((2,)), dma((2,)), dma((2,)), dma((2, 10)),
        ],
        compiler_params=pltpu.CompilerParams(
            collective_id=0, has_side_effects=True, vmem_limit_bytes=60 * 1024 * 1024
        ),
    )(inputs, cotangent, right_weight, left_weight, first_gate, second_gate)
    return out, gi, gr, gl, gf, gs


def solution(mesh):
    placed = (P("seq", None, "ch"), P(None, "seq", "ch"), P(), P(), P(None, "ch"), P(None, "ch"))
    return jax.shard_map(
        functools.partial(per_device, mesh.shape["seq"], mesh.shape["ch"]),
        mesh=mesh,
        in_specs=placed,
        out_specs=(
            P(None, "seq", "ch"),
            P("seq", None, "ch"),
            P(("seq", "ch"), None),
            P(("seq", "ch"), None),
            P("seq", "ch"),
            P("seq", "ch"),
        ),
        check_vma=False,
    )
```

time: 431 us -> 138 us (0.32)
  waiting for transfers between devices: 293 us -> 0 us
  Pallas kernels: 0 us -> 129 us
  local copies, waits for them, and re-layouts: 45.7 us -> 6.92 us
  blocking collectives: 22.5 us -> 0 us
  matrix products: 22 us -> 0 us
  starting transfers between devices: 21 us -> 0 us
  between operations: 14.9 us -> 0.67 us
  other arithmetic: 10.4 us -> 0 us
    unnamed x4 -> x0, waiting for transfers between devices: 208 us -> none
    pallas_call x0 -> x1, Pallas kernels: none -> 129 us  [per_device(): pl.pallas_call(functools.partial(fused, seqs, chs, grid), out_shape=(jax....]
    all_to_all x2 -> x0, waiting for transfers between devices: 84.9 us -> none  [the longest x1 44.4 us: per_device(): lax.all_to_all(panels, 'seq', split_axis=1, concat_axis=0, tiled=True)]
    unnamed x1 -> x0, blocking collectives: 22.5 us -> none
    dot_general x6 -> x0, matrix products: 22 us -> none  [the longest x1 5.52 us: per_device(): jnp.einsum('mi,ikd->mkd', left_weight, received, preferred_element_type=j...]
    all_to_all x2 -> x0, starting transfers between devices: 20.7 us -> none  [the longest x1 12.4 us: per_device(): lax.all_to_all(panels, 'seq', split_axis=1, concat_axis=0, tiled=True)]
    unnamed x31 -> x16, local copies, waits for them, and re-layouts: 23.5 us -> 6.92 us
    convert_element_type x5 -> x0, local copies, waits for them, and re-layouts: 15.8 us -> none  [the longest x1 5.4 us: per_device(): returned32 = returned.astype(jnp.float32)]
  transfers between devices with their start and end apart: 4 -> 0, of which waited for: 4 -> 0; matrix products, arithmetic and copies ran while one was open for 11% -> 0% of each run, Pallas kernels for 0% -> 0%
where the time goes in v2:
time: 138 us; the launch traced here: 137 us
  Pallas kernels  129 us (93%)
  local copies, waits for them, and re-layouts  6.92 us (5%)
    pallas_call x1, Pallas kernels, per_device(): pl.pallas_call(functools.partial(fused, seqs, chs, grid), out_shape=(jax....  129 us
    unnamed x16, local copies, waits for them, and re-layouts  6.92 us

profile of v2, /device:TPU:24, one launch (start us, length us, event | category | flops | bytes accessed | tf_op | source)
XLA Modules:
  0.0 136.9 jit_solution(382154200796330589)
XLA Ops:
  0.6 129.4 %shard_map.109 = (bf16[512,8,256]{2,1,0:T(8,128)(2,1)}, bf16[8,512,256]{2,1,0:T(8,128)(2,1)}, f32[2,512]{1,0:T(2,128)}, f32[2,512]{1,0:T(2,128)}, f32[8,256]{1,0:T(8,128)}, /*index=5*/f32[8,256]{1,0:T(8,128)}) custom-call(bf16[8,512,256]{2,1,0:T(8,128)(2,1)} %x_hbm.1, bf16[512,8,256]{2,1,0:T(8,128)(2,1)} %ct_hbm.1, bf16[512,512]{1,0:T(8,128)(2,1)} %right_hbm.1, ...), custom_call_target="tpu_custom_call" | custom-call | tf_op jit(solution)/shard_map/pallas_call | solution.py:321
  130.0 0.0 copy-start
  130.0 3.2 %copy.18 = bf16[512,8,256]{2,1,0:T(8,128)(2,1)} copy(bf16[512,8,256]{2,1,0:T(8,128)(2,1)} %get-tuple-element.12) | data formatting | bytes 4194304
  133.2 0.0 copy-done
  133.2 0.0 copy-start.4
  133.2 0.0 copy-start.3
  133.2 0.0 copy-start.2
  133.2 0.0 copy-start.1
  133.2 1.3 copy.19
  134.5 0.0 copy-done.4
  134.5 0.6 copy.20
  135.1 0.0 copy-done.3
  135.1 0.6 copy.21
  135.7 0.0 copy-done.2
  135.7 0.6 copy.22
  136.3 0.0 copy-done.1
  136.3 0.6 copy.23
Async XLA Ops:
  130.0 3.2 %copy-start = (bf16[8,512,256]{2,1,0:T(8,128)(2,1)S(1)}, bf16[8,512,256]{2,1,0:T(8,128)(2,1)}, u32[]{:S(2)}) copy-start(bf16[8,512,256]{2,1,0:T(8,128)(2,1)} %get-tuple-element.13) | copy-start | bytes 6291460
  133.2 1.3 copy-start.4
  133.2 1.9 %copy-start.3 = (f32[2,512]{1,0:T(2,128)S(1)}, f32[2,512]{1,0:T(2,128)}, u32[]{:S(2)}) copy-start(f32[2,512]{1,0:T(2,128)} %get-tuple-element.15) | copy-start | bytes 12292
  133.2 2.5 %copy-start.2 = (f32[8,256]{1,0:T(8,128)S(1)}, f32[8,256]{1,0:T(8,128)}, u32[]{:S(2)}) copy-start(f32[8,256]{1,0:T(8,128)} %get-tuple-element.16) | copy-start | bytes 24580
  133.2 3.1 %copy-start.1 = (f32[8,256]{1,0:T(8,128)S(1)}, f32[8,256]{1,0:T(8,128)}, u32[]{:S(2)}) copy-start(f32[8,256]{1,0:T(8,128)} %get-tuple-element.17) | copy-start | bytes 24580

commit v3 on v2

v3 whole, which is shorter than its diff:
```python
import functools

import jax
import jax.numpy as jnp
from jax import lax
from jax.experimental import pallas as pl
from jax.experimental.pallas import tpu as pltpu
from jax.sharding import PartitionSpec as P

MESH = pl.DeviceIdType.MESH
F32 = jnp.float32
BF16 = jnp.bfloat16
LANES = 128
ROWS = 64
CHIPS_Z = 8
LIMIT_MIB = 44


def dot(a, b, contract):
    return lax.dot_general(a, b, ((contract[:1], contract[1:]), ((), ())), preferred_element_type=F32)


def fused(
    seqs, zs, chs, grid,
    x_hbm, ct_hbm, right_hbm, left_hbm, gate1_hbm, gate2_hbm,
    ov, giv, gr_out, gl_out, gf_out, gs_out,
    xv, ctv, right, left, gate1, gate2,
    right_t, left_t, s1, flat, flat_out, prod, pair, grad_pair, section, gl, gr, gfirst, gsecond,
    fsend, frecv, bsend, brecv,
    csend, crecv, cgsend, cgrecv, half, xsend, xrecv, ysend, yrecv, ygsend, ygrecv, thin, zsend, zrecv, zgsend, zgrecv,
    in_sem, fs_sem, fr_sem, bs_sem, br_sem, r_sem,
):
    s, ch = lax.axis_index("seq"), lax.axis_index("ch")
    core = s % 2
    own_y, own_z = s // (2 * zs), (s // 2) % zs
    ys = seqs // (2 * zs)
    pairs = seqs // 2
    blocks = grid // ROWS

    barrier = pltpu.get_barrier_semaphore()

    def greet(t, _):
        pl.semaphore_signal(barrier, inc=1, device_id=((s + t) % seqs, ch), device_id_type=MESH)
        return 0

    def greet_ch(t, _):
        pl.semaphore_signal(barrier, inc=1, device_id=(s, (ch + t) % chs), device_id_type=MESH)
        return 0

    loads = [
        pltpu.make_async_copy(src, dst, in_sem.at[n])
        for n, (src, dst) in enumerate(
            ((x_hbm, xv), (right_hbm, right), (gate1_hbm, gate1), (ct_hbm, ctv), (left_hbm, left), (gate2_hbm, gate2))
        )
    ]
    for load in loads:
        load.start()
    lax.fori_loop(1, seqs, greet, 0)
    lax.fori_loop(1, chs, greet_ch, 0)
    for load in loads[:3]:
        load.wait()

    def half_of(h):
        return slice(h * LANES, (h + 1) * LANES)

    def x_pair(h, ip):
        return jnp.concatenate([xv[2 * ip, :, half_of(h)], xv[2 * ip + 1, :, half_of(h)]], axis=1)

    def turn(n, extent):
        odd = n % 2
        return (odd * ((n + 1) // 2) + (1 - odd) * (extent - n // 2)) % extent

    def far_first(t):
        z = (own_z + turn(t % zs, zs)) % zs
        y = (own_y + turn(t // zs % ys, ys)) % ys
        return (y * zs + z) * 2 + (core + t // (zs * ys)) % 2

    def exchange(h, src, dst, send_sem, recv_sem):
        pltpu.make_async_copy(src.at[h, s], dst.at[h, s], recv_sem.at[h]).start()

        def send(t, _):
            d = far_first(seqs - t)
            pltpu.make_async_remote_copy(
                src_ref=src.at[h, d], dst_ref=dst.at[h, s], send_sem=send_sem.at[h], recv_sem=recv_sem.at[h],
                device_id=(d, ch), device_id_type=MESH,
            ).start()
            return 0

        lax.fori_loop(1, seqs, send, 0)

    def arrived(dst, sem):
        pltpu.make_async_copy(dst, dst, sem).wait()

    def first_stage(h):
        def per_pair(ip, _):
            prod[...] = dot(right[...], x_pair(h, ip), (1, 0))

            def rows(b, _):
                r = pl.ds(pl.multiple_of(b * ROWS, ROWS), ROWS)
                gate = gate1[r, half_of(h)].astype(F32)
                for e in range(2):
                    rounded = prod[r, half_of(e)].astype(BF16)
                    s1[2 * ip + e, h, r, :] = rounded
                    flat[pl.ds(b * (ROWS * 8) + 2 * ip + e, ROWS, stride=8), :] = rounded.astype(F32) * gate
                return 0

            lax.fori_loop(0, blocks, rows, 0)
            return 0

        lax.fori_loop(0, 4, per_pair, 0)

        def pack(d, _):
            rows = flat[pl.ds(pl.multiple_of(d * 64, 64), 64), :]
            fsend[h, d] = rows.reshape(8, 8, LANES).astype(BF16)
            return 0

        lax.fori_loop(0, seqs, pack, 0, unroll=4)

    def middle(h):
        def unpack(b, _):
            m = pl.ds(pl.multiple_of(b * 8, 8), 8)
            flat[pl.ds(pl.multiple_of(b * 64, 64), 64), :] = ctv[m, :, half_of(h)].astype(F32).reshape(64, LANES)
            return 0

        lax.fori_loop(0, grid // 8, unpack, 0, unroll=4)
        gsecond[:, half_of(h)] = jnp.zeros((grid, LANES), F32)
        arrived(frecv.at[h], fr_sem.at[h])

        def per_pair(kp, _):
            pair[...] = jnp.concatenate(
                [frecv[h, :, 2 * kp + e].astype(F32).reshape(grid, LANES).astype(BF16) for e in range(2)], axis=1
            )
            prod[...] = dot(left[...], pair[...], (1, 0))

            def rows(b, _):
                r = pl.ds(pl.multiple_of(b * ROWS, ROWS), ROWS)
                gate = gate2[r, half_of(h)].astype(F32)
                total = gsecond[r, half_of(h)]
                for e in range(2):
                    at = pl.ds(b * (ROWS * 8) + 2 * kp + e, ROWS, stride=8)
                    mixed = prod[r, half_of(e)]
                    grad_out = flat[at, :]
                    logistic = 1.0 / (1.0 + jnp.exp(-mixed))
                    activated = mixed * logistic
                    flat_out[at, :] = activated * gate
                    total = total + grad_out * activated
                    grad_mixed = grad_out * gate * logistic * (1.0 + mixed * (1.0 - logistic))
                    grad_pair[r, half_of(e)] = grad_mixed.astype(BF16)
                gsecond[r, half_of(h)] = total
                return 0

            lax.fori_loop(0, blocks, rows, 0)
            gl[...] += dot(grad_pair[...], pair[...], (1, 1))
            prod[...] = dot(left_t[...], grad_pair[...], (1, 0))
            for e in range(2):
                bsend[h, :, 2 * kp + e] = prod[:, half_of(e)].reshape(seqs, 8, LANES).astype(BF16)
            return 0

        lax.fori_loop(0, 4, per_pair, 0)

    def write_out(h):
        def pack(b, _):
            m = pl.ds(pl.multiple_of(b * 8, 8), 8)
            rows = flat_out[pl.ds(pl.multiple_of(b * 64, 64), 64), :]
            ov[m, :, half_of(h)] = rows.reshape(8, 8, LANES).astype(BF16)
            return 0

        lax.fori_loop(0, grid // 8, pack, 0, unroll=4)

    def last_stage(h):
        gfirst[:, half_of(h)] = jnp.zeros((grid, LANES), F32)
        arrived(brecv.at[h], br_sem.at[h])

        def unpack(b, _):
            rows = brecv[h, b].astype(F32).reshape(64, LANES)
            flat[pl.ds(pl.multiple_of(b * 64, 64), 64), :] = rows
            return 0

        lax.fori_loop(0, seqs, unpack, 0, unroll=4)

        def per_pair(ip, _):
            def rows(b, _):
                r = pl.ds(pl.multiple_of(b * ROWS, ROWS), ROWS)
                gate = gate1[r, half_of(h)].astype(F32)
                total = gfirst[r, half_of(h)]
                for e in range(2):
                    grad = flat[pl.ds(b * (ROWS * 8) + 2 * ip + e, ROWS, stride=8), :]
                    total = total + grad * s1[2 * ip + e, h, r, :].astype(F32)
                    section[ip, r, half_of(e)] = (grad * gate).astype(BF16)
                gfirst[r, half_of(h)] = total
                return 0

            lax.fori_loop(0, blocks, rows, 0)
            gr[...] += dot(section[ip], x_pair(h, ip), (1, 1))
            return 0

        lax.fori_loop(0, 4, per_pair, 0)

    def grad_of_inputs(h):
        def per_pair(ip, _):
            prod[...] = dot(right_t[...], section[ip], (1, 0))
            for e in range(2):
                giv[2 * ip + e, :, half_of(h)] = prod[:, half_of(e)].astype(BF16)
            return 0

        lax.fori_loop(0, 4, per_pair, 0)

    def to_peers(count, me, src, dst, send_sem, recv_sem, device):
        pltpu.make_async_copy(src.at[me], dst.at[me], recv_sem).start()
        for t in range(1, count):
            d = (me + t) % count
            pltpu.make_async_remote_copy(
                src_ref=src.at[d], dst_ref=dst.at[me], send_sem=send_sem, recv_sem=recv_sem,
                device_id=device(d), device_id_type=MESH,
            ).start()

    def at_ch(d):
        return (s, d)

    def at_y(d):
        return ((d * zs + own_z) * 2 + core, ch)

    def at_z(d):
        return ((own_y * zs + d) * 2 + core, ch)

    def core_copies(n):
        return [
            pltpu.make_async_remote_copy(
                src_ref=src.at[n], dst_ref=dst.at[n], send_sem=r_sem.at[n, 2 * q], recv_sem=r_sem.at[n, 2 * q + 1],
                device_id=(s + 1 - 2 * core, ch), device_id_type=MESH,
            )
            for q, (src, dst) in enumerate(((csend, crecv), (cgsend, cgrecv)))
        ]

    def reduce_core(n, matrix, gates):
        def give(p, _):
            r = pl.ds(pl.multiple_of(p * 16 + (1 - core) * 8, 8), 8)
            csend[n, p] = matrix[r, :].astype(BF16)
            cgsend[n, p] = gates[r, :].astype(BF16)
            return 0

        lax.fori_loop(0, pairs, give, 0, unroll=4)
        for copy in core_copies(n):
            copy.start()

    def reduce_ch(n, matrix, gates):
        for copy in core_copies(n):
            copy.wait()

        def take(p, _):
            r = pl.ds(pl.multiple_of(p * 16 + core * 8, 8), 8)
            total = matrix[r, :] + crecv[n, p].astype(F32)
            for c in range(4):
                half[c, pl.ds(pl.multiple_of(p * 8, 8), 8), :] = total[:, c * LANES : (c + 1) * LANES]
            ygsend[n, p // zs, p % zs] = (gates[r, :] + cgrecv[n, p].astype(F32)).astype(BF16)
            return 0

        lax.fori_loop(0, pairs, take, 0, unroll=4)
        for a in range(chs):
            for b in range(2):
                for c in range(4):
                    lanes = slice(c * LANES, (c + 1) * LANES)
                    xsend[n, a, b, :, lanes] = half[c, pl.ds(2 * a + b, pairs, stride=8), :].astype(BF16)
        to_peers(chs, ch, xsend.at[n], xrecv.at[n], r_sem.at[n, 4], r_sem.at[n, 5], at_ch)
        to_peers(ys, own_y, ygsend.at[n], ygrecv.at[n], r_sem.at[n, 6], r_sem.at[n, 7], at_y)

    def reduce_y(n):
        arrived(xrecv.at[n], r_sem.at[n, 5])
        total = xrecv[n, 0].astype(F32)
        for a in range(1, chs):
            total = total + xrecv[n, a].astype(F32)
        for a in range(ys):
            ysend[n, a] = total[:, a * zs : (a + 1) * zs].astype(BF16)
        to_peers(ys, own_y, ysend.at[n], yrecv.at[n], r_sem.at[n, 8], r_sem.at[n, 9], at_y)

    def reduce_z_gates(n):
        arrived(ygrecv.at[n], r_sem.at[n, 7])
        total = ygrecv[n, 0].astype(F32)
        for a in range(1, ys):
            total = total + ygrecv[n, a].astype(F32)
        zgsend[n] = total.astype(BF16)
        to_peers(zs, own_z, zgsend.at[n], zgrecv.at[n], r_sem.at[n, 10], r_sem.at[n, 11], at_z)

    def reduce_z(n):
        arrived(yrecv.at[n], r_sem.at[n, 9])
        total = yrecv[n, 0].astype(F32)
        for a in range(1, ys):
            total = total + yrecv[n, a].astype(F32)
        total = total.reshape(2 * zs, grid)
        for c in range(4):
            thin[c] = total[:, c * LANES : (c + 1) * LANES]
        for p in range(zs):
            for c in range(4):
                zsend[n, p, :, c * LANES : (c + 1) * LANES] = thin[c, pl.ds(p, 2, stride=zs), :].astype(BF16)
        to_peers(zs, own_z, zsend.at[n], zrecv.at[n], r_sem.at[n, 12], r_sem.at[n, 13], at_z)

    def finish(n, matrix_out, gates_out):
        arrived(zgrecv.at[n], r_sem.at[n, 11])
        gates_out[...] = jnp.sum(zgrecv[n].astype(F32), axis=0)
        arrived(zrecv.at[n], r_sem.at[n, 13])
        matrix_out[...] = jnp.sum(zrecv[n].astype(F32), axis=0)
        for buffer, count, sem in (
            (xsend, chs, 4), (ygsend, ys, 6), (ysend, ys, 8), (zgsend, zs, 10), (zsend, zs, 12)
        ):
            arrived(buffer.at[n, pl.ds(0, count - 1)], r_sem.at[n, sem])

    first_stage(0)
    pl.semaphore_wait(barrier, seqs + chs - 2)
    exchange(0, fsend, frecv, fs_sem, fr_sem)
    first_stage(1)
    exchange(1, fsend, frecv, fs_sem, fr_sem)
    for load in loads[3:]:
        load.wait()
    right_t[...] = right[...].T
    left_t[...] = left[...].T
    gl[...] = jnp.zeros(gl.shape, F32)
    gr[...] = jnp.zeros(gr.shape, F32)
    for h in range(2):
        middle(h)
        exchange(h, bsend, brecv, bs_sem, br_sem)
        if h == 1:
            reduce_core(0, gl, gsecond)
        write_out(h)
    reduce_ch(0, gl, gsecond)
    reduce_y(0)
    last_stage(0)
    grad_of_inputs(0)
    last_stage(1)
    reduce_core(1, gr, gfirst)
    reduce_z_gates(0)
    reduce_z(0)
    grad_of_inputs(1)
    reduce_ch(1, gr, gfirst)
    reduce_z_gates(1)
    reduce_y(1)
    reduce_z(1)
    finish(0, gl_out, gs_out)
    finish(1, gr_out, gf_out)
    for h in range(2):
        arrived(fsend.at[h, pl.ds(0, seqs - 1)], fs_sem.at[h])
        arrived(bsend.at[h, pl.ds(0, seqs - 1)], bs_sem.at[h])


def place(*refs):
    count = len(refs) // 2
    sems = refs[-1]
    copies = [pltpu.make_async_copy(refs[q], refs[count + q], sems.at[q]) for q in range(count)]
    for copy in copies:
        copy.start()
    for copy in copies:
        copy.wait()


def per_device(seqs, zs, chs, inputs, cotangent, right_weight, left_weight, first_gate, second_gate):
    rows, grid, width = inputs.shape
    any_space = pl.BlockSpec(memory_space=pl.ANY)
    hbm = pl.BlockSpec(memory_space=pltpu.HBM)
    vmem = pl.BlockSpec(memory_space=pltpu.VMEM)
    pairs, ys = seqs // 2, seqs // (2 * zs)
    block = (2, seqs, 8, 8, LANES)

    def v(shape, dtype=BF16):
        return pltpu.VMEM(shape, dtype)

    def twice(*shape):
        return [pltpu.VMEM((2,) + shape, BF16)] * 2

    dma = pltpu.SemaphoreType.DMA
    shapes = (
        jax.ShapeDtypeStruct(cotangent.shape, BF16),
        jax.ShapeDtypeStruct(inputs.shape, BF16),
        jax.ShapeDtypeStruct((2, grid), F32),
        jax.ShapeDtypeStruct((2, grid), F32),
        jax.ShapeDtypeStruct((8, width), F32),
        jax.ShapeDtypeStruct((8, width), F32),
    )
    results = pl.pallas_call(
        functools.partial(fused, seqs, zs, chs, grid),
        out_shape=shapes,
        in_specs=[hbm] * 6,
        out_specs=(vmem,) * 6,
        scratch_shapes=[
            v(inputs.shape), v(cotangent.shape), v((grid, grid)), v((grid, grid)), v((grid, width)), v((grid, width)),
            v((grid, grid)), v((grid, grid)), v((8, 2, grid, LANES)), v((grid * 8, LANES), F32), v((grid * 8, LANES), F32),
            v((grid, 2 * LANES), F32), v((grid, 2 * LANES)), v((grid, 2 * LANES)), v((4, grid, 2 * LANES)),
            v((grid, grid), F32), v((grid, grid), F32), v((grid, width), F32), v((grid, width), F32),
            v(block), v(block), v(block), v(block),
            *twice(pairs, 8, grid), *twice(pairs, 8, width),
            v((4, pairs * 8, LANES), F32), *twice(chs, 2, pairs, grid),
            *twice(ys, 2, zs, grid), *twice(ys, zs, 8, width),
            v((4, 2 * zs, LANES), F32), *twice(zs, 2, grid), *twice(zs, 8, width),
            dma((6,)), dma((2,)), dma((2,)), dma((2,)), dma((2,)), dma((2, 14)),
        ],
        compiler_params=pltpu.CompilerParams(
            collective_id=0, has_side_effects=True, vmem_limit_bytes=LIMIT_MIB * 1024 * 1024
        ),
    )(*(
        pltpu.with_memory_space_constraint(array, pltpu.HBM)
        for array in (inputs, cotangent, right_weight, left_weight, first_gate, second_gate)
    ))
    return pl.pallas_call(
        place,
        out_shape=shapes,
        in_specs=[any_space] * 6,
        out_specs=(hbm,) * 6,
        scratch_shapes=[dma((6,))],
        compiler_params=pltpu.CompilerParams(vmem_limit_bytes=4 * 1024 * 1024),
    )(*results)


def solution(mesh):
    placed = (P("seq", None, "ch"), P(None, "seq", "ch"), P(), P(), P(None, "ch"), P(None, "ch"))
    return jax.shard_map(
        functools.partial(per_device, mesh.shape["seq"], CHIPS_Z, mesh.shape["ch"]),
        mesh=mesh,
        in_specs=placed,
        out_specs=(
            P(None, "seq", "ch"),
            P("seq", None, "ch"),
            P(("seq", "ch"), None),
            P(("seq", "ch"), None),
            P("seq", "ch"),
            P("seq", "ch"),
        ),
        check_vma=False,
    )
```

time: 138 us -> 125 us (0.906)
  local copies, waits for them, and re-layouts: 6.92 us -> 0 us
  Pallas kernels: 129 us -> 124 us
    unnamed x16 -> x0, local copies, waits for them, and re-layouts: 6.92 us -> none
    pallas_call x1 -> x2, Pallas kernels: 129 us -> 124 us  [the longest x1 121 us: per_device(): pl.pallas_call(functools.partial(fused, seqs, zs, chs, grid), out_shape=s...]
where the time goes in v3:
time: 125 us; the launch traced here: 124 us
  Pallas kernels  124 us (99%)
    pallas_call x1, Pallas kernels, per_device(): pl.pallas_call(functools.partial(fused, seqs, zs, chs, grid), out_shape=s...  121 us

profile of v3, /device:TPU:24, one launch (start us, length us, event | category | flops | bytes accessed | tf_op | source)
XLA Modules:
  0.0 124.2 jit_solution(11571771774419297856)
XLA Ops:
  0.6 121.5 %shard_map.109 = (bf16[512,8,256]{2,1,0:T(8,128)(2,1)S(1)}, bf16[8,512,256]{2,1,0:T(8,128)(2,1)S(1)}, f32[2,512]{1,0:T(2,128)S(1)}, f32[2,512]{1,0:T(2,128)S(1)}...) custom-call(bf16[8,512,256]{2,1,0:T(8,128)(2,1)} %x_hbm.1, bf16[512,8,256]{2,1,0:T(8,128)(2,1)} %ct_hbm.1, ...), custom_call_target="tpu_custom_call" | custom-call | tf_op jit(solution)/shard_map/pallas_call | solution.py:377
  122.1 2.1 %shard_map.110 = (bf16[512,8,256]{2,1,0:T(8,128)(2,1)}, bf16[8,512,256]{2,1,0:T(8,128)(2,1)}, f32[2,512]{1,0:T(2,128)}, f32[2,512]{1,0:T(2,128)}, f32[8,256]{1,0:T(8,128)}, /*index=5*/f32[8,256]{1,0:T(8,128)}) custom-call(bf16[512,8,256]{2,1,0:T(8,128)(2,1)S(1)} %get-tuple-element.12.refs_0_, bf16[8,512,256]{2,1,0:T(8,128)(2,1)S(1)} %get-tuple-element.13.refs_1_, ...), custom_call_target="tpu_custom_call" | custom-call | tf_op jit(solution)/shard_map/pallas_call | solution.py:401

commit v4 on v3

--- a/solution.py
+++ b/solution.py
@@ -25,14 +25,14 @@
     x_hbm, ct_hbm, right_hbm, left_hbm, gate1_hbm, gate2_hbm,
     ov, giv, gr_out, gl_out, gf_out, gs_out,
     xv, ctv, right, left, gate1, gate2,
-    right_t, left_t, s1, flat, flat_out, prod, pair, grad_pair, section, gl, gr, gfirst, gsecond,
+    right_t, left_t, gate1_p, s1, flat, flat_out, prod, pair, grad_pair, section, gl, gr, gfirst, gsecond,
     fsend, frecv, bsend, brecv,
-    csend, crecv, cgsend, cgrecv, half, xsend, xrecv, ysend, yrecv, ygsend, ygrecv, thin, zsend, zrecv, zgsend, zgrecv,
+    csend, crecv, cgsend, cgrecv, half, xysend, xyrecv, ygsend, ygrecv, thin, zsend, zrecv, zgsend, zgrecv,
     in_sem, fs_sem, fr_sem, bs_sem, br_sem, r_sem,
 ):
     s, ch = lax.axis_index("seq"), lax.axis_index("ch")
     core = s % 2
-    own_y, own_z = s // (2 * zs), (s // 2) % zs
+    own, own_y, own_z = s // 2, s // (2 * zs), (s // 2) % zs
     ys = seqs // (2 * zs)
     pairs = seqs // 2
     blocks = grid // ROWS
@@ -44,7 +44,8 @@
         return 0
 
     def greet_ch(t, _):
-        pl.semaphore_signal(barrier, inc=1, device_id=(s, (ch + t) % chs), device_id_type=MESH)
+        x, y = (ch + 1 + t // ys) % chs, t % ys
+        pl.semaphore_signal(barrier, inc=1, device_id=((y * zs + own_z) * 2 + core, x), device_id_type=MESH)
         return 0
 
     loads = [
@@ -56,7 +57,7 @@
     for load in loads:
         load.start()
     lax.fori_loop(1, seqs, greet, 0)
-    lax.fori_loop(1, chs, greet_ch, 0)
+    lax.fori_loop(0, (chs - 1) * ys, greet_ch, 0)
     for load in loads[:3]:
         load.wait()
 
@@ -75,18 +76,33 @@
         y = (own_y + turn(t // zs % ys, ys)) % ys
         return (y * zs + z) * 2 + (core + t // (zs * ys)) % 2
 
-    def exchange(h, src, dst, send_sem, recv_sem):
-        pltpu.make_async_copy(src.at[h, s], dst.at[h, s], recv_sem.at[h]).start()
+    def spread(h):
+        pltpu.make_async_copy(fsend.at[h, s], frecv.at[h, s], fr_sem.at[h]).start()
 
         def send(t, _):
             d = far_first(seqs - t)
             pltpu.make_async_remote_copy(
-                src_ref=src.at[h, d], dst_ref=dst.at[h, s], send_sem=send_sem.at[h], recv_sem=recv_sem.at[h],
+                src_ref=fsend.at[h, d], dst_ref=frecv.at[h, s], send_sem=fs_sem.at[h], recv_sem=fr_sem.at[h],
                 device_id=(d, ch), device_id_type=MESH,
             ).start()
             return 0
 
         lax.fori_loop(1, seqs, send, 0)
+
+    def send_back(h):
+        pltpu.make_async_copy(bsend.at[h, s], brecv.at[h, core, own], br_sem.at[h, 1]).start()
+        for rel, first, last in ((0, 1, pairs + 1), (1, pairs + 1, seqs)):
+
+            def send(t, _):
+                d = far_first(seqs - t)
+                pltpu.make_async_remote_copy(
+                    src_ref=bsend.at[h, d], dst_ref=brecv.at[h, core, own],
+                    send_sem=bs_sem.at[h], recv_sem=br_sem.at[h, rel],
+                    device_id=(d, ch), device_id_type=MESH,
+                ).start()
+                return 0
+
+            lax.fori_loop(first, last, send, 0)
 
     def arrived(dst, sem):
         pltpu.make_async_copy(dst, dst, sem).wait()
@@ -99,9 +115,12 @@
                 r = pl.ds(pl.multiple_of(b * ROWS, ROWS), ROWS)
                 gate = gate1[r, half_of(h)].astype(F32)
                 for e in range(2):
-                    rounded = prod[r, half_of(e)].astype(BF16)
-                    s1[2 * ip + e, h, r, :] = rounded
-                    flat[pl.ds(b * (ROWS * 8) + 2 * ip + e, ROWS, stride=8), :] = rounded.astype(F32) * gate
+                    rounded = prod[r, half_of(e)].astype(BF16).astype(F32)
+                    flat[pl.ds(b * (ROWS * 8) + 2 * ip + e, ROWS, stride=8), :] = rounded * gate
+                    rounded = rounded.reshape(ROWS // 16, 2, 8, LANES)
+                    to = pl.ds(pl.multiple_of(b * (ROWS // 2), ROWS // 2), ROWS // 2)
+                    for p in range(2):
+                        s1[2 * ip + e, h, p, to, :] = rounded[:, p].reshape(ROWS // 2, LANES).astype(BF16)
                 return 0
 
             lax.fori_loop(0, blocks, rows, 0)
@@ -167,38 +186,41 @@
 
         lax.fori_loop(0, grid // 8, pack, 0, unroll=4)
 
-    def last_stage(h):
-        gfirst[:, half_of(h)] = jnp.zeros((grid, LANES), F32)
-        arrived(brecv.at[h], br_sem.at[h])
+    def parity(rel):
+        return core if rel else 1 - core
+
+    def last_stage(h, rel):
+        p = parity(rel)
+        arrived(brecv.at[h, p], br_sem.at[h, rel])
 
         def unpack(b, _):
-            rows = brecv[h, b].astype(F32).reshape(64, LANES)
+            rows = brecv[h, p, b].astype(F32).reshape(64, LANES)
             flat[pl.ds(pl.multiple_of(b * 64, 64), 64), :] = rows
             return 0
 
-        lax.fori_loop(0, seqs, unpack, 0, unroll=4)
+        lax.fori_loop(0, pairs, unpack, 0, unroll=4)
 
         def per_pair(ip, _):
             def rows(b, _):
                 r = pl.ds(pl.multiple_of(b * ROWS, ROWS), ROWS)
-                gate = gate1[r, half_of(h)].astype(F32)
-                total = gfirst[r, half_of(h)]
+                gate = gate1_p[p, r, half_of(h)]
+                total = gfirst[p, r, half_of(h)]
                 for e in range(2):
                     grad = flat[pl.ds(b * (ROWS * 8) + 2 * ip + e, ROWS, stride=8), :]
-                    total = total + grad * s1[2 * ip + e, h, r, :].astype(F32)
-                    section[ip, r, half_of(e)] = (grad * gate).astype(BF16)
-                gfirst[r, half_of(h)] = total
+                    total = total + grad * s1[2 * ip + e, h, p, r, :].astype(F32)
+                    section[p, ip, r, half_of(e)] = (grad * gate).astype(BF16)
+                gfirst[p, r, half_of(h)] = total
                 return 0
 
-            lax.fori_loop(0, blocks, rows, 0)
-            gr[...] += dot(section[ip], x_pair(h, ip), (1, 1))
+            lax.fori_loop(0, blocks // 2, rows, 0)
+            gr[p] += dot(section[p, ip], x_pair(h, ip), (1, 1))
             return 0
 
         lax.fori_loop(0, 4, per_pair, 0)
 
     def grad_of_inputs(h):
         def per_pair(ip, _):
-            prod[...] = dot(right_t[...], section[ip], (1, 0))
+            prod[...] = dot(right_t[0], section[0, ip], (1, 0)) + dot(right_t[1], section[1, ip], (1, 0))
             for e in range(2):
                 giv[2 * ip + e, :, half_of(h)] = prod[:, half_of(e)].astype(BF16)
             return 0
@@ -214,8 +236,8 @@
                 device_id=device(d), device_id_type=MESH,
             ).start()
 
-    def at_ch(d):
-        return (s, d)
+    def at_xy(d):
+        return ((d % ys * zs + own_z) * 2 + core, d // ys)
 
     def at_y(d):
         return ((d * zs + own_z) * 2 + core, ch)
@@ -232,27 +254,25 @@
             for q, (src, dst) in enumerate(((csend, crecv), (cgsend, cgrecv)))
         ]
 
-    def reduce_core(n, matrix, gates):
-        def give(p, _):
-            r = pl.ds(pl.multiple_of(p * 16 + (1 - core) * 8, 8), 8)
-            csend[n, p] = matrix[r, :].astype(BF16)
-            cgsend[n, p] = gates[r, :].astype(BF16)
+    def reduce_core(n, rows):
+        def give(q, _):
+            csend[n, q], cgsend[n, q] = (part.astype(BF16) for part in rows(1 - core, q))
             return 0
 
         lax.fori_loop(0, pairs, give, 0, unroll=4)
         for copy in core_copies(n):
             copy.start()
 
-    def reduce_ch(n, matrix, gates):
+    def reduce_xy(n, rows):
         for copy in core_copies(n):
             copy.wait()
 
-        def take(p, _):
-            r = pl.ds(pl.multiple_of(p * 16 + core * 8, 8), 8)
-            total = matrix[r, :] + crecv[n, p].astype(F32)
+        def take(q, _):
+            matrix, gates = rows(core, q)
+            total = matrix + crecv[n, q].astype(F32)
             for c in range(4):
-                half[c, pl.ds(pl.multiple_of(p * 8, 8), 8), :] = total[:, c * LANES : (c + 1) * LANES]
-            ygsend[n, p // zs, p % zs] = (gates[r, :] + cgrecv[n, p].astype(F32)).astype(BF16)
+                half[c, pl.ds(pl.multiple_of(q * 8, 8), 8), :] = total[:, c * LANES : (c + 1) * LANES]
+            ygsend[n, q // zs, q % zs] = (gates + cgrecv[n, q].astype(F32)).astype(BF16)
             return 0
 
         lax.fori_loop(0, pairs, take, 0, unroll=4)
@@ -260,18 +280,11 @@
             for b in range(2):
                 for c in range(4):
                     lanes = slice(c * LANES, (c + 1) * LANES)
-                    xsend[n, a, b, :, lanes] = half[c, pl.ds(2 * a + b, pairs, stride=8), :].astype(BF16)
-        to_peers(chs, ch, xsend.at[n], xrecv.at[n], r_sem.at[n, 4], r_sem.at[n, 5], at_ch)
+                    part = half[c, pl.ds(2 * a + b, pairs, stride=8), :]
+                    for y in range(ys):
+                        xysend[n, a * ys + y, b, :, lanes] = part[y * zs : (y + 1) * zs].astype(BF16)
+        to_peers(chs * ys, ch * ys + own_y, xysend.at[n], xyrecv.at[n], r_sem.at[n, 4], r_sem.at[n, 5], at_xy)
         to_peers(ys, own_y, ygsend.at[n], ygrecv.at[n], r_sem.at[n, 6], r_sem.at[n, 7], at_y)
-
-    def reduce_y(n):
-        arrived(xrecv.at[n], r_sem.at[n, 5])
-        total = xrecv[n, 0].astype(F32)
-        for a in range(1, chs):
-            total = total + xrecv[n, a].astype(F32)
-        for a in range(ys):
-            ysend[n, a] = total[:, a * zs : (a + 1) * zs].astype(BF16)
-        to_peers(ys, own_y, ysend.at[n], yrecv.at[n], r_sem.at[n, 8], r_sem.at[n, 9], at_y)
 
     def reduce_z_gates(n):
         arrived(ygrecv.at[n], r_sem.at[n, 7])
@@ -279,60 +292,79 @@
         for a in range(1, ys):
             total = total + ygrecv[n, a].astype(F32)
         zgsend[n] = total.astype(BF16)
-        to_peers(zs, own_z, zgsend.at[n], zgrecv.at[n], r_sem.at[n, 10], r_sem.at[n, 11], at_z)
+        to_peers(zs, own_z, zgsend.at[n], zgrecv.at[n], r_sem.at[n, 8], r_sem.at[n, 9], at_z)
 
     def reduce_z(n):
-        arrived(yrecv.at[n], r_sem.at[n, 9])
-        total = yrecv[n, 0].astype(F32)
-        for a in range(1, ys):
-            total = total + yrecv[n, a].astype(F32)
+        arrived(xyrecv.at[n], r_sem.at[n, 5])
+        total = xyrecv[n, 0].astype(F32)
+        for a in range(1, chs * ys):
+            total = total + xyrecv[n, a].astype(F32)
         total = total.reshape(2 * zs, grid)
         for c in range(4):
             thin[c] = total[:, c * LANES : (c + 1) * LANES]
         for p in range(zs):
             for c in range(4):
                 zsend[n, p, :, c * LANES : (c + 1) * LANES] = thin[c, pl.ds(p, 2, stride=zs), :].astype(BF16)
-        to_peers(zs, own_z, zsend.at[n], zrecv.at[n], r_sem.at[n, 12], r_sem.at[n, 13], at_z)
+        to_peers(zs, own_z, zsend.at[n], zrecv.at[n], r_sem.at[n, 10], r_sem.at[n, 11], at_z)
 
     def finish(n, matrix_out, gates_out):
-        arrived(zgrecv.at[n], r_sem.at[n, 11])
+        arrived(zgrecv.at[n], r_sem.at[n, 9])
         gates_out[...] = jnp.sum(zgrecv[n].astype(F32), axis=0)
-        arrived(zrecv.at[n], r_sem.at[n, 13])
+        arrived(zrecv.at[n], r_sem.at[n, 11])
         matrix_out[...] = jnp.sum(zrecv[n].astype(F32), axis=0)
         for buffer, count, sem in (
-            (xsend, chs, 4), (ygsend, ys, 6), (ysend, ys, 8), (zgsend, zs, 10), (zsend, zs, 12)
+            (xysend, chs * ys, 4), (ygsend, ys, 6), (zgsend, zs, 8), (zsend, zs, 10)
         ):
             arrived(buffer.at[n, pl.ds(0, count - 1)], r_sem.at[n, sem])
 
+    def left_rows(p, q):
+        r = pl.ds(pl.multiple_of(q * 16 + p * 8, 8), 8)
+        return gl[r, :], gsecond[r, :]
+
+    def right_rows_of(p, q):
+        r = pl.ds(pl.multiple_of(q * 8, 8), 8)
+        return gr[p, r, :], gfirst[p, r, :]
+
     first_stage(0)
-    pl.semaphore_wait(barrier, seqs + chs - 2)
-    exchange(0, fsend, frecv, fs_sem, fr_sem)
+    pl.semaphore_wait(barrier, seqs - 1 + (chs - 1) * ys)
+    spread(0)
     first_stage(1)
-    exchange(1, fsend, frecv, fs_sem, fr_sem)
+    spread(1)
     for load in loads[3:]:
         load.wait()
-    right_t[...] = right[...].T
+    right_rows = right[...].astype(F32).reshape(pairs, 2, 8, grid)
+    for p in range(2):
+        right_t[p] = right_rows[:, p].reshape(grid // 2, grid).astype(BF16).T
+
+    def split_gate(q, _):
+        rows = gate1[pl.ds(pl.multiple_of(q * 16, 16), 16), :].astype(F32)
+        for p in range(2):
+            gate1_p[p, pl.ds(pl.multiple_of(q * 8, 8), 8), :] = rows[p * 8 : p * 8 + 8]
+        return 0
+
+    lax.fori_loop(0, pairs, split_gate, 0)
+    gfirst[...] = jnp.zeros(gfirst.shape, F32)
     left_t[...] = left[...].T
     gl[...] = jnp.zeros(gl.shape, F32)
     gr[...] = jnp.zeros(gr.shape, F32)
     for h in range(2):
         middle(h)
-        exchange(h, bsend, brecv, bs_sem, br_sem)
+        send_back(h)
         if h == 1:
-            reduce_core(0, gl, gsecond)
+            reduce_core(0, left_rows)
         write_out(h)
-    reduce_ch(0, gl, gsecond)
-    reduce_y(0)
-    last_stage(0)
+    reduce_xy(0, left_rows)
+    last_stage(0, 0)
+    last_stage(0, 1)
     grad_of_inputs(0)
-    last_stage(1)
-    reduce_core(1, gr, gfirst)
+    last_stage(1, 0)
+    reduce_core(1, right_rows_of)
     reduce_z_gates(0)
     reduce_z(0)
+    last_stage(1, 1)
+    reduce_xy(1, right_rows_of)
     grad_of_inputs(1)
-    reduce_ch(1, gr, gfirst)
     reduce_z_gates(1)
-    reduce_y(1)
     reduce_z(1)
     finish(0, gl_out, gs_out)
     finish(1, gr_out, gf_out)
@@ -381,15 +413,15 @@
         out_specs=(vmem,) * 6,
         scratch_shapes=[
             v(inputs.shape), v(cotangent.shape), v((grid, grid)), v((grid, grid)), v((grid, width)), v((grid, width)),
-            v((grid, grid)), v((grid, grid)), v((8, 2, grid, LANES)), v((grid * 8, LANES), F32), v((grid * 8, LANES), F32),
-            v((grid, 2 * LANES), F32), v((grid, 2 * LANES)), v((grid, 2 * LANES)), v((4, grid, 2 * LANES)),
-            v((grid, grid), F32), v((grid, grid), F32), v((grid, width), F32), v((grid, width), F32),
-            v(block), v(block), v(block), v(block),
+            v((2, grid, grid // 2)), v((grid, grid)), v((2, grid // 2, width), F32), v((8, 2, 2, grid // 2, LANES)), v((grid * 8, LANES), F32), v((grid * 8, LANES), F32),
+            v((grid, 2 * LANES), F32), v((grid, 2 * LANES)), v((grid, 2 * LANES)), v((2, 4, grid // 2, 2 * LANES)),
+            v((grid, grid), F32), v((2, grid // 2, grid), F32), v((2, grid // 2, width), F32), v((grid, width), F32),
+            v(block), v(block), v(block), v((2, 2, pairs, 8, 8, LANES)),
             *twice(pairs, 8, grid), *twice(pairs, 8, width),
-            v((4, pairs * 8, LANES), F32), *twice(chs, 2, pairs, grid),
-            *twice(ys, 2, zs, grid), *twice(ys, zs, 8, width),
+            v((4, pairs * 8, LANES), F32), *twice(chs * ys, 2, zs, grid),
+            *twice(ys, zs, 8, width),
             v((4, 2 * zs, LANES), F32), *twice(zs, 2, grid), *twice(zs, 8, width),
-            dma((6,)), dma((2,)), dma((2,)), dma((2,)), dma((2,)), dma((2, 14)),
+            dma((6,)), dma((2,)), dma((2,)), dma((2,)), dma((2, 2)), dma((2, 12)),
         ],
         compiler_params=pltpu.CompilerParams(
             collective_id=0, has_side_effects=True, vmem_limit_bytes=LIMIT_MIB * 1024 * 1024

time: 125 us -> 119 us (0.952)
  Pallas kernels: 124 us -> 119 us
    pallas_call x1, Pallas kernels: 121 us -> 116 us  [per_device(): pl.pallas_call(functools.partial(fused, seqs, zs, chs, grid), out_shape=s...]
where the time goes in v4:
time: 119 us
  Pallas kernels  119 us (100%)
    pallas_call x1, Pallas kernels, per_device(): pl.pallas_call(functools.partial(fused, seqs, zs, chs, grid), out_shape=s...  116 us

profile of v4, /device:TPU:24, one launch (start us, length us, event | category | flops | bytes accessed | tf_op | source)
XLA Modules:
  0.0 119.2 jit_solution(3391741246456012433)
XLA Ops:
  0.6 116.5 %shard_map.109 = (bf16[512,8,256]{2,1,0:T(8,128)(2,1)S(1)}, bf16[8,512,256]{2,1,0:T(8,128)(2,1)S(1)}, f32[2,512]{1,0:T(2,128)S(1)}, f32[2,512]{1,0:T(2,128)S(1)}...) custom-call(bf16[8,512,256]{2,1,0:T(8,128)(2,1)} %x_hbm.1, bf16[512,8,256]{2,1,0:T(8,128)(2,1)} %ct_hbm.1, ...), custom_call_target="tpu_custom_call" | custom-call | tf_op jit(solution)/shard_map/pallas_call | solution.py:409
  117.1 2.1 %shard_map.110 = (bf16[512,8,256]{2,1,0:T(8,128)(2,1)}, bf16[8,512,256]{2,1,0:T(8,128)(2,1)}, f32[2,512]{1,0:T(2,128)}, f32[2,512]{1,0:T(2,128)}, f32[8,256]{1,0:T(8,128)}, /*index=5*/f32[8,256]{1,0:T(8,128)}) custom-call(bf16[512,8,256]{2,1,0:T(8,128)(2,1)S(1)} %get-tuple-element.12.refs_0_, bf16[8,512,256]{2,1,0:T(8,128)(2,1)S(1)} %get-tuple-element.13.refs_1_, ...), custom_call_target="tpu_custom_call" | custom-call | tf_op jit(solution)/shard_map/pallas_call | solution.py:433

commit v5 on v4

--- a/solution.py
+++ b/solution.py
@@ -39,8 +39,17 @@
 
     barrier = pltpu.get_barrier_semaphore()
 
+    def turn(n, extent):
+        odd = n % 2
+        return (odd * ((n + 1) // 2) + (1 - odd) * (extent - n // 2)) % extent
+
+    def far_first(t):
+        z = (own_z + turn(t % zs, zs)) % zs
+        y = (own_y + turn(t // zs % ys, ys)) % ys
+        return (y * zs + z) * 2 + (core + t // (zs * ys)) % 2
+
     def greet(t, _):
-        pl.semaphore_signal(barrier, inc=1, device_id=((s + t) % seqs, ch), device_id_type=MESH)
+        pl.semaphore_signal(barrier, inc=1, device_id=(far_first(seqs - t), ch), device_id_type=MESH)
         return 0
 
     def greet_ch(t, _):
@@ -54,10 +63,12 @@
             ((x_hbm, xv), (right_hbm, right), (gate1_hbm, gate1), (ct_hbm, ctv), (left_hbm, left), (gate2_hbm, gate2))
         )
     ]
-    for load in loads:
+    for load in loads[:3]:
         load.start()
     lax.fori_loop(1, seqs, greet, 0)
     lax.fori_loop(0, (chs - 1) * ys, greet_ch, 0)
+    for load in loads[3:]:
+        load.start()
     for load in loads[:3]:
         load.wait()
 
@@ -66,15 +77,6 @@
 
     def x_pair(h, ip):
         return jnp.concatenate([xv[2 * ip, :, half_of(h)], xv[2 * ip + 1, :, half_of(h)]], axis=1)
-
-    def turn(n, extent):
-        odd = n % 2
-        return (odd * ((n + 1) // 2) + (1 - odd) * (extent - n // 2)) % extent
-
-    def far_first(t):
-        z = (own_z + turn(t % zs, zs)) % zs
-        y = (own_y + turn(t // zs % ys, ys)) % ys
-        return (y * zs + z) * 2 + (core + t // (zs * ys)) % 2
 
     def spread(h):
         pltpu.make_async_copy(fsend.at[h, s], frecv.at[h, s], fr_sem.at[h]).start()
@@ -90,14 +92,16 @@
         lax.fori_loop(1, seqs, send, 0)
 
     def send_back(h):
-        pltpu.make_async_copy(bsend.at[h, s], brecv.at[h, core, own], br_sem.at[h, 1]).start()
-        for rel, first, last in ((0, 1, pairs + 1), (1, pairs + 1, seqs)):
+        pltpu.make_async_copy(bsend.at[h, s], brecv.at[h, core, own], br_sem.at[h, ys]).start()
+        for part, first, last in [(0, 1, pairs + 1)] + [
+            (v + 1, pairs + 1 + v * zs, min(pairs + 1 + (v + 1) * zs, seqs)) for v in range(ys)
+        ]:
 
             def send(t, _):
                 d = far_first(seqs - t)
                 pltpu.make_async_remote_copy(
                     src_ref=bsend.at[h, d], dst_ref=brecv.at[h, core, own],
-                    send_sem=bs_sem.at[h], recv_sem=br_sem.at[h, rel],
+                    send_sem=bs_sem.at[h], recv_sem=br_sem.at[h, part],
                     device_id=(d, ch), device_id_type=MESH,
                 ).start()
                 return 0
@@ -186,23 +190,28 @@
 
         lax.fori_loop(0, grid // 8, pack, 0, unroll=4)
 
-    def parity(rel):
-        return core if rel else 1 - core
-
-    def last_stage(h, rel):
-        p = parity(rel)
-        arrived(brecv.at[h, p], br_sem.at[h, rel])
-
+    def y_of_part(part):
+        return (own_y + ys - turn(ys - part, ys)) % ys
+
+    def rows_arrived(h, part):
+        if part == 0:
+            arrived(brecv.at[h, 1 - core], br_sem.at[h, 0])
+        else:
+            y = y_of_part(part)
+            arrived(brecv.at[h, core, pl.ds(y * zs, zs)], br_sem.at[h, part])
+
+    def last_stage(h, p, y, count):
         def unpack(b, _):
-            rows = brecv[h, p, b].astype(F32).reshape(64, LANES)
+            rows = brecv[h, p, y * zs + b].astype(F32).reshape(64, LANES)
             flat[pl.ds(pl.multiple_of(b * 64, 64), 64), :] = rows
             return 0
 
-        lax.fori_loop(0, pairs, unpack, 0, unroll=4)
+        lax.fori_loop(0, count * zs, unpack, 0, unroll=4)
+        whole = pl.ds(pl.multiple_of(y * ROWS, ROWS), count * ROWS)
 
         def per_pair(ip, _):
             def rows(b, _):
-                r = pl.ds(pl.multiple_of(b * ROWS, ROWS), ROWS)
+                r = pl.ds(pl.multiple_of((y + b) * ROWS, ROWS), ROWS)
                 gate = gate1_p[p, r, half_of(h)]
                 total = gfirst[p, r, half_of(h)]
                 for e in range(2):
@@ -212,8 +221,8 @@
                 gfirst[p, r, half_of(h)] = total
                 return 0
 
-            lax.fori_loop(0, blocks // 2, rows, 0)
-            gr[p] += dot(section[p, ip], x_pair(h, ip), (1, 1))
+            lax.fori_loop(0, count, rows, 0)
+            gr[p, whole, :] += dot(section[p, ip, whole, :], x_pair(h, ip), (1, 1))
             return 0
 
         lax.fori_loop(0, 4, per_pair, 0)
@@ -236,12 +245,6 @@
                 device_id=device(d), device_id_type=MESH,
             ).start()
 
-    def at_xy(d):
-        return ((d % ys * zs + own_z) * 2 + core, d // ys)
-
-    def at_y(d):
-        return ((d * zs + own_z) * 2 + core, ch)
-
     def at_z(d):
         return ((own_y * zs + d) * 2 + core, ch)
 
@@ -263,28 +266,44 @@
         for copy in core_copies(n):
             copy.start()
 
-    def reduce_xy(n, rows):
+    def core_arrived(n):
         for copy in core_copies(n):
             copy.wait()
 
-        def take(q, _):
+    def reduce_xy(n, rows, y, mine):
+        def take(z, _):
+            q = y * zs + z
             matrix, gates = rows(core, q)
             total = matrix + crecv[n, q].astype(F32)
             for c in range(4):
                 half[c, pl.ds(pl.multiple_of(q * 8, 8), 8), :] = total[:, c * LANES : (c + 1) * LANES]
-            ygsend[n, q // zs, q % zs] = (gates + cgrecv[n, q].astype(F32)).astype(BF16)
-            return 0
-
-        lax.fori_loop(0, pairs, take, 0, unroll=4)
+            ygsend[n, y, z] = (gates + cgrecv[n, q].astype(F32)).astype(BF16)
+            return 0
+
+        lax.fori_loop(0, zs, take, 0, unroll=4)
         for a in range(chs):
             for b in range(2):
                 for c in range(4):
-                    lanes = slice(c * LANES, (c + 1) * LANES)
-                    part = half[c, pl.ds(2 * a + b, pairs, stride=8), :]
-                    for y in range(ys):
-                        xysend[n, a * ys + y, b, :, lanes] = part[y * zs : (y + 1) * zs].astype(BF16)
-        to_peers(chs * ys, ch * ys + own_y, xysend.at[n], xyrecv.at[n], r_sem.at[n, 4], r_sem.at[n, 5], at_xy)
-        to_peers(ys, own_y, ygsend.at[n], ygrecv.at[n], r_sem.at[n, 6], r_sem.at[n, 7], at_y)
+                    part = half[c, pl.ds(y * (8 * zs) + 2 * a + b, zs, stride=8), :]
+                    xysend[n, a * ys + y, b, :, c * LANES : (c + 1) * LANES] = part.astype(BF16)
+        to = ch * ys + own_y
+        for t in range(chs):
+            d = (ch + t) % chs
+            if mine and t == 0:
+                pltpu.make_async_copy(xysend.at[n, to], xyrecv.at[n, to], r_sem.at[n, 5]).start()
+            else:
+                pltpu.make_async_remote_copy(
+                    src_ref=xysend.at[n, d * ys + y], dst_ref=xyrecv.at[n, to],
+                    send_sem=r_sem.at[n, 4], recv_sem=r_sem.at[n, 5],
+                    device_id=((y * zs + own_z) * 2 + core, d), device_id_type=MESH,
+                ).start()
+        if mine:
+            pltpu.make_async_copy(ygsend.at[n, y], ygrecv.at[n, y], r_sem.at[n, 7]).start()
+        else:
+            pltpu.make_async_remote_copy(
+                src_ref=ygsend.at[n, y], dst_ref=ygrecv.at[n, own_y], send_sem=r_sem.at[n, 6], recv_sem=r_sem.at[n, 7],
+                device_id=((y * zs + own_z) * 2 + core, ch), device_id_type=MESH,
+            ).start()
 
     def reduce_z_gates(n):
         arrived(ygrecv.at[n], r_sem.at[n, 7])
@@ -353,20 +372,29 @@
         if h == 1:
             reduce_core(0, left_rows)
         write_out(h)
-    reduce_xy(0, left_rows)
-    last_stage(0, 0)
-    last_stage(0, 1)
+    core_arrived(0)
+    for part in range(1, ys + 1):
+        reduce_xy(0, left_rows, y_of_part(part), part == ys)
+    rows_arrived(0, 0)
+    last_stage(0, 1 - core, 0, ys)
+    for part in range(1, ys + 1):
+        rows_arrived(0, part)
+    last_stage(0, core, 0, ys)
     grad_of_inputs(0)
-    last_stage(1, 0)
+    rows_arrived(1, 0)
+    last_stage(1, 1 - core, 0, ys)
     reduce_core(1, right_rows_of)
     reduce_z_gates(0)
     reduce_z(0)
-    last_stage(1, 1)
-    reduce_xy(1, right_rows_of)
+    core_arrived(1)
+    for part in range(1, ys + 1):
+        rows_arrived(1, part)
+        last_stage(1, core, y_of_part(part), 1)
+        reduce_xy(1, right_rows_of, y_of_part(part), part == ys)
     grad_of_inputs(1)
+    finish(0, gl_out, gs_out)
     reduce_z_gates(1)
     reduce_z(1)
-    finish(0, gl_out, gs_out)
     finish(1, gr_out, gf_out)
     for h in range(2):
         arrived(fsend.at[h, pl.ds(0, seqs - 1)], fs_sem.at[h])
@@ -421,7 +449,7 @@
             v((4, pairs * 8, LANES), F32), *twice(chs * ys, 2, zs, grid),
             *twice(ys, zs, 8, width),
             v((4, 2 * zs, LANES), F32), *twice(zs, 2, grid), *twice(zs, 8, width),
-            dma((6,)), dma((2,)), dma((2,)), dma((2,)), dma((2, 2)), dma((2, 12)),
+            dma((6,)), dma((2,)), dma((2,)), dma((2,)), dma((2, ys + 1)), dma((2, 12)),
         ],
         compiler_params=pltpu.CompilerParams(
             collective_id=0, has_side_effects=True, vmem_limit_bytes=LIMIT_MIB * 1024 * 1024

time: 119 us -> 118 us (level)
  Pallas kernels: 119 us -> 117 us
    pallas_call x1, Pallas kernels: 116 us -> 115 us  [per_device(): pl.pallas_call(functools.partial(fused, seqs, zs, chs, grid), out_shape=s...]
where the time goes in v5:
time: 118 us; the launch traced here: 117 us
  Pallas kernels  117 us (99%)
    pallas_call x1, Pallas kernels, per_device(): pl.pallas_call(functools.partial(fused, seqs, zs, chs, grid), out_shape=s...  115 us

profile of v5, /device:TPU:24, one launch (start us, length us, event | category | flops | bytes accessed | tf_op | source)
XLA Modules:
  0.0 117.4 jit_solution(14169767769985778589)
XLA Ops:
  0.6 114.7 %shard_map.109 = (bf16[512,8,256]{2,1,0:T(8,128)(2,1)S(1)}, bf16[8,512,256]{2,1,0:T(8,128)(2,1)S(1)}, f32[2,512]{1,0:T(2,128)S(1)}, f32[2,512]{1,0:T(2,128)S(1)}...) custom-call(bf16[8,512,256]{2,1,0:T(8,128)(2,1)} %x_hbm.1, bf16[512,8,256]{2,1,0:T(8,128)(2,1)} %ct_hbm.1, ...), custom_call_target="tpu_custom_call" | custom-call | tf_op jit(solution)/shard_map/pallas_call | solution.py:437
  115.4 2.1 %shard_map.110 = (bf16[512,8,256]{2,1,0:T(8,128)(2,1)}, bf16[8,512,256]{2,1,0:T(8,128)(2,1)}, f32[2,512]{1,0:T(2,128)}, f32[2,512]{1,0:T(2,128)}, f32[8,256]{1,0:T(8,128)}, /*index=5*/f32[8,256]{1,0:T(8,128)}) custom-call(bf16[512,8,256]{2,1,0:T(8,128)(2,1)S(1)} %get-tuple-element.12.refs_0_, bf16[8,512,256]{2,1,0:T(8,128)(2,1)S(1)} %get-tuple-element.13.refs_1_, ...), custom_call_target="tpu_custom_call" | custom-call | tf_op jit(solution)/shard_map/pallas_call | solution.py:461

commit v6 on v4

--- a/solution.py
+++ b/solution.py
@@ -39,9 +39,25 @@
 
     barrier = pltpu.get_barrier_semaphore()
 
-    def greet(t, _):
-        pl.semaphore_signal(barrier, inc=1, device_id=((s + t) % seqs, ch), device_id_type=MESH)
-        return 0
+    def turns(extent):
+        return [(n + 1) // 2 if n % 2 else extent - n // 2 for n in reversed(range(1, extent))] + [0]
+
+    def sweep(act, cores):
+        far_z, far_y = turns(zs), turns(ys)
+        for other in cores:
+            c = 1 - core if other else core
+
+            def row(y, offsets):
+                base = y * (2 * zs) + c
+                for dz in offsets:
+                    act(base + 2 * lax.rem(own_z + dz, zs))
+
+            for dy in far_y[:-1]:
+                row(lax.rem(own_y + dy, ys), far_z)
+            row(own_y, far_z if other else far_z[:-1])
+
+    def greet(d):
+        pl.semaphore_signal(barrier, inc=1, device_id=(d, ch), device_id_type=MESH)
 
     def greet_ch(t, _):
         x, y = (ch + 1 + t // ys) % chs, t % ys
@@ -56,7 +72,7 @@
     ]
     for load in loads:
         load.start()
-    lax.fori_loop(1, seqs, greet, 0)
+    sweep(greet, (True, False))
     lax.fori_loop(0, (chs - 1) * ys, greet_ch, 0)
     for load in loads[:3]:
         load.wait()
@@ -67,42 +83,29 @@
     def x_pair(h, ip):
         return jnp.concatenate([xv[2 * ip, :, half_of(h)], xv[2 * ip + 1, :, half_of(h)]], axis=1)
 
-    def turn(n, extent):
-        odd = n % 2
-        return (odd * ((n + 1) // 2) + (1 - odd) * (extent - n // 2)) % extent
-
-    def far_first(t):
-        z = (own_z + turn(t % zs, zs)) % zs
-        y = (own_y + turn(t // zs % ys, ys)) % ys
-        return (y * zs + z) * 2 + (core + t // (zs * ys)) % 2
-
     def spread(h):
         pltpu.make_async_copy(fsend.at[h, s], frecv.at[h, s], fr_sem.at[h]).start()
 
-        def send(t, _):
-            d = far_first(seqs - t)
+        def send(d):
             pltpu.make_async_remote_copy(
                 src_ref=fsend.at[h, d], dst_ref=frecv.at[h, s], send_sem=fs_sem.at[h], recv_sem=fr_sem.at[h],
                 device_id=(d, ch), device_id_type=MESH,
             ).start()
-            return 0
-
-        lax.fori_loop(1, seqs, send, 0)
+
+        sweep(send, (True, False))
 
     def send_back(h):
         pltpu.make_async_copy(bsend.at[h, s], brecv.at[h, core, own], br_sem.at[h, 1]).start()
-        for rel, first, last in ((0, 1, pairs + 1), (1, pairs + 1, seqs)):
-
-            def send(t, _):
-                d = far_first(seqs - t)
+        for rel in range(2):
+
+            def send(d):
                 pltpu.make_async_remote_copy(
                     src_ref=bsend.at[h, d], dst_ref=brecv.at[h, core, own],
                     send_sem=bs_sem.at[h], recv_sem=br_sem.at[h, rel],
                     device_id=(d, ch), device_id_type=MESH,
                 ).start()
-                return 0
-
-            lax.fori_loop(first, last, send, 0)
+
+            sweep(send, (rel == 0,))
 
     def arrived(dst, sem):
         pltpu.make_async_copy(dst, dst, sem).wait()
@@ -198,7 +201,7 @@
             flat[pl.ds(pl.multiple_of(b * 64, 64), 64), :] = rows
             return 0
 
-        lax.fori_loop(0, pairs, unpack, 0, unroll=4)
+        lax.fori_loop(0, pairs, unpack, 0, unroll=8)
 
         def per_pair(ip, _):
             def rows(b, _):
@@ -212,11 +215,11 @@
                 gfirst[p, r, half_of(h)] = total
                 return 0
 
-            lax.fori_loop(0, blocks // 2, rows, 0)
+            lax.fori_loop(0, blocks // 2, rows, 0, unroll=True)
             gr[p] += dot(section[p, ip], x_pair(h, ip), (1, 1))
             return 0
 
-        lax.fori_loop(0, 4, per_pair, 0)
+        lax.fori_loop(0, 4, per_pair, 0, unroll=True)
 
     def grad_of_inputs(h):
         def per_pair(ip, _):
@@ -225,7 +228,7 @@
                 giv[2 * ip + e, :, half_of(h)] = prod[:, half_of(e)].astype(BF16)
             return 0
 
-        lax.fori_loop(0, 4, per_pair, 0)
+        lax.fori_loop(0, 4, per_pair, 0, unroll=True)
 
     def to_peers(count, me, src, dst, send_sem, recv_sem, device):
         pltpu.make_async_copy(src.at[me], dst.at[me], recv_sem).start()
@@ -275,7 +278,7 @@
             ygsend[n, q // zs, q % zs] = (gates + cgrecv[n, q].astype(F32)).astype(BF16)
             return 0
 
-        lax.fori_loop(0, pairs, take, 0, unroll=4)
+        lax.fori_loop(0, pairs, take, 0, unroll=8)
         for a in range(chs):
             for b in range(2):
                 for c in range(4):
@@ -376,7 +379,15 @@
 def place(*refs):
     count = len(refs) // 2
     sems = refs[-1]
-    copies = [pltpu.make_async_copy(refs[q], refs[count + q], sems.at[q]) for q in range(count)]
+    copies = []
+    for q in range(count):
+        cuts = 4 if q < 2 else 1
+        rows = refs[q].shape[0] // cuts
+        for n in range(cuts):
+            at = pl.ds(n * rows, rows)
+            copies.append(
+                pltpu.make_async_copy(refs[q].at[at], refs[count + q].at[at], sems.at[len(copies)])
+            )
     for copy in copies:
         copy.start()
     for copy in copies:
@@ -435,7 +446,7 @@
         out_shape=shapes,
         in_specs=[any_space] * 6,
         out_specs=(hbm,) * 6,
-        scratch_shapes=[dma((6,))],
+        scratch_shapes=[dma((12,))],
         compiler_params=pltpu.CompilerParams(vmem_limit_bytes=4 * 1024 * 1024),
     )(*results)
 

time: 119 us -> 118 us (level)
  Pallas kernels: 119 us -> 117 us
    pallas_call x1, Pallas kernels: 116 us -> 115 us  [per_device(): pl.pallas_call(functools.partial(fused, seqs, zs, chs, grid), out_shape=s...]
where the time goes in v6:
time: 118 us
  Pallas kernels  117 us (99%)
    pallas_call x1, Pallas kernels, per_device(): pl.pallas_call(functools.partial(fused, seqs, zs, chs, grid), out_shape=s...  115 us

profile of v6, /device:TPU:24, one launch (start us, length us, event | category | flops | bytes accessed | tf_op | source)
XLA Modules:
  0.0 118.0 jit_solution(14926075843106725780)
XLA Ops:
  0.6 115.3 %shard_map.109 = (bf16[512,8,256]{2,1,0:T(8,128)(2,1)S(1)}, bf16[8,512,256]{2,1,0:T(8,128)(2,1)S(1)}, f32[2,512]{1,0:T(2,128)S(1)}, f32[2,512]{1,0:T(2,128)S(1)}...) custom-call(bf16[8,512,256]{2,1,0:T(8,128)(2,1)} %x_hbm.1, bf16[512,8,256]{2,1,0:T(8,128)(2,1)} %ct_hbm.1, ...), custom_call_target="tpu_custom_call" | custom-call | tf_op jit(solution)/shard_map/pallas_call | solution.py:420
  115.9 2.1 %shard_map.110 = (bf16[512,8,256]{2,1,0:T(8,128)(2,1)}, bf16[8,512,256]{2,1,0:T(8,128)(2,1)}, f32[2,512]{1,0:T(2,128)}, f32[2,512]{1,0:T(2,128)}, f32[8,256]{1,0:T(8,128)}, /*index=5*/f32[8,256]{1,0:T(8,128)}) custom-call(bf16[512,8,256]{2,1,0:T(8,128)(2,1)S(1)} %get-tuple-element.12.refs_0_, bf16[8,512,256]{2,1,0:T(8,128)(2,1)S(1)} %get-tuple-element.13.refs_1_, ...), custom_call_target="tpu_custom_call" | custom-call | tf_op jit(solution)/shard_map/pallas_call | solution.py:444

commit v7 on v6

--- a/solution.py
+++ b/solution.py
@@ -36,25 +36,29 @@
     ys = seqs // (2 * zs)
     pairs = seqs // 2
     blocks = grid // ROWS
+    quads, part_rows = seqs // 4, grid // 4
+    z_class = own_z % 2
 
     barrier = pltpu.get_barrier_semaphore()
 
     def turns(extent):
         return [(n + 1) // 2 if n % 2 else extent - n // 2 for n in reversed(range(1, extent))] + [0]
 
-    def sweep(act, cores):
-        far_z, far_y = turns(zs), turns(ys)
-        for other in cores:
-            c = 1 - core if other else core
-
-            def row(y, offsets):
-                base = y * (2 * zs) + c
-                for dz in offsets:
-                    act(base + 2 * lax.rem(own_z + dz, zs))
-
-            for dy in far_y[:-1]:
-                row(lax.rem(own_y + dy, ys), far_z)
-            row(own_y, far_z if other else far_z[:-1])
+    def sweep(act, other, offsets):
+        far_y = turns(ys)
+        c = 1 - core if other else core
+
+        def row(y, distances):
+            base = y * (2 * zs) + c
+            for dz in distances:
+                act(base + 2 * lax.rem(own_z + dz, zs))
+
+        for dy in far_y[:-1]:
+            row(lax.rem(own_y + dy, ys), offsets)
+        row(own_y, offsets if other else [dz for dz in offsets if dz])
+
+    far_z = turns(zs)
+    odd_z, even_z = [dz for dz in far_z if dz % 2], [dz for dz in far_z if dz % 2 == 0]
 
     def greet(d):
         pl.semaphore_signal(barrier, inc=1, device_id=(d, ch), device_id_type=MESH)
@@ -72,7 +76,8 @@
     ]
     for load in loads:
         load.start()
-    sweep(greet, (True, False))
+    for other in (True, False):
+        sweep(greet, other, far_z)
     lax.fori_loop(0, (chs - 1) * ys, greet_ch, 0)
     for load in loads[:3]:
         load.wait()
@@ -92,20 +97,24 @@
                 device_id=(d, ch), device_id_type=MESH,
             ).start()
 
-        sweep(send, (True, False))
-
-    def send_back(h):
-        pltpu.make_async_copy(bsend.at[h, s], brecv.at[h, core, own], br_sem.at[h, 1]).start()
-        for rel in range(2):
+        for other in (True, False):
+            sweep(send, other, far_z)
+
+    def send_back(h, parts):
+        mine = z_class * quads + s // 4
+        if 2 in parts:
+            pltpu.make_async_copy(bsend.at[h, s], brecv.at[h, core, mine], br_sem.at[h, 2]).start()
+        for part in parts:
+            other, offsets = ((True, far_z), (False, odd_z), (False, even_z))[part]
 
             def send(d):
                 pltpu.make_async_remote_copy(
-                    src_ref=bsend.at[h, d], dst_ref=brecv.at[h, core, own],
-                    send_sem=bs_sem.at[h], recv_sem=br_sem.at[h, rel],
+                    src_ref=bsend.at[h, d], dst_ref=brecv.at[h, core, mine],
+                    send_sem=bs_sem.at[h], recv_sem=br_sem.at[h, part],
                     device_id=(d, ch), device_id_type=MESH,
                 ).start()
 
-            sweep(send, (rel == 0,))
+            sweep(send, other, offsets)
 
     def arrived(dst, sem):
         pltpu.make_async_copy(dst, dst, sem).wait()
@@ -120,10 +129,11 @@
                 for e in range(2):
                     rounded = prod[r, half_of(e)].astype(BF16).astype(F32)
                     flat[pl.ds(b * (ROWS * 8) + 2 * ip + e, ROWS, stride=8), :] = rounded * gate
-                    rounded = rounded.reshape(ROWS // 16, 2, 8, LANES)
-                    to = pl.ds(pl.multiple_of(b * (ROWS // 2), ROWS // 2), ROWS // 2)
-                    for p in range(2):
-                        s1[2 * ip + e, h, p, to, :] = rounded[:, p].reshape(ROWS // 2, LANES).astype(BF16)
+                    rounded = rounded.reshape(ROWS // 32, 2, 2, 8, LANES)
+                    for zp in range(2):
+                        to = pl.ds(pl.multiple_of(zp * part_rows + b * (ROWS // 4), ROWS // 4), ROWS // 4)
+                        for p in range(2):
+                            s1[2 * ip + e, h, p, to, :] = rounded[:, zp, p].reshape(ROWS // 4, LANES).astype(BF16)
                 return 0
 
             lax.fori_loop(0, blocks, rows, 0)
@@ -189,23 +199,28 @@
 
         lax.fori_loop(0, grid // 8, pack, 0, unroll=4)
 
-    def parity(rel):
-        return core if rel else 1 - core
-
-    def last_stage(h, rel):
-        p = parity(rel)
-        arrived(brecv.at[h, p], br_sem.at[h, rel])
-
+    def class_of(order):
+        return z_class if order else 1 - z_class
+
+    def rows_arrived(h, part):
+        if part == 0:
+            arrived(brecv.at[h, 1 - core], br_sem.at[h, 0])
+        else:
+            at = pl.ds(class_of(part - 1) * quads, quads)
+            arrived(brecv.at[h, core, at], br_sem.at[h, part])
+
+    def last_stage(h, p, first, count):
         def unpack(b, _):
-            rows = brecv[h, p, b].astype(F32).reshape(64, LANES)
+            rows = brecv[h, p, first * quads + b].astype(F32).reshape(64, LANES)
             flat[pl.ds(pl.multiple_of(b * 64, 64), 64), :] = rows
             return 0
 
-        lax.fori_loop(0, pairs, unpack, 0, unroll=8)
+        lax.fori_loop(0, count * quads, unpack, 0, unroll=8)
+        whole = pl.ds(pl.multiple_of(first * part_rows, part_rows), count * part_rows)
 
         def per_pair(ip, _):
             def rows(b, _):
-                r = pl.ds(pl.multiple_of(b * ROWS, ROWS), ROWS)
+                r = pl.ds(pl.multiple_of(first * part_rows + b * ROWS, ROWS), ROWS)
                 gate = gate1_p[p, r, half_of(h)]
                 total = gfirst[p, r, half_of(h)]
                 for e in range(2):
@@ -215,8 +230,8 @@
                 gfirst[p, r, half_of(h)] = total
                 return 0
 
-            lax.fori_loop(0, blocks // 2, rows, 0, unroll=True)
-            gr[p] += dot(section[p, ip], x_pair(h, ip), (1, 1))
+            lax.fori_loop(0, count * part_rows // ROWS, rows, 0, unroll=True)
+            gr[p, whole, :] += dot(section[p, ip, whole, :], x_pair(h, ip), (1, 1))
             return 0
 
         lax.fori_loop(0, 4, per_pair, 0, unroll=True)
@@ -266,28 +281,33 @@
         for copy in core_copies(n):
             copy.start()
 
-    def reduce_xy(n, rows):
+    def core_arrived(n):
         for copy in core_copies(n):
             copy.wait()
 
-        def take(q, _):
+    def reduce_xy(n, rows, order):
+        def take(q2, _):
+            q = 2 * q2 + class_of(order)
             matrix, gates = rows(core, q)
             total = matrix + crecv[n, q].astype(F32)
             for c in range(4):
-                half[c, pl.ds(pl.multiple_of(q * 8, 8), 8), :] = total[:, c * LANES : (c + 1) * LANES]
+                half[c, pl.ds(pl.multiple_of(q2 * 8, 8), 8), :] = total[:, c * LANES : (c + 1) * LANES]
             ygsend[n, q // zs, q % zs] = (gates + cgrecv[n, q].astype(F32)).astype(BF16)
             return 0
 
-        lax.fori_loop(0, pairs, take, 0, unroll=8)
+        lax.fori_loop(0, quads, take, 0, unroll=8)
         for a in range(chs):
-            for b in range(2):
-                for c in range(4):
-                    lanes = slice(c * LANES, (c + 1) * LANES)
-                    part = half[c, pl.ds(2 * a + b, pairs, stride=8), :]
-                    for y in range(ys):
-                        xysend[n, a * ys + y, b, :, lanes] = part[y * zs : (y + 1) * zs].astype(BF16)
-        to_peers(chs * ys, ch * ys + own_y, xysend.at[n], xyrecv.at[n], r_sem.at[n, 4], r_sem.at[n, 5], at_xy)
-        to_peers(ys, own_y, ygsend.at[n], ygrecv.at[n], r_sem.at[n, 6], r_sem.at[n, 7], at_y)
+            for y in range(ys):
+                for b in range(2):
+                    for c in range(4):
+                        part = half[c, pl.ds(y * (4 * zs) + 2 * a + b, zs // 2, stride=8), :]
+                        xysend[n, order, a * ys + y, b, :, c * LANES : (c + 1) * LANES] = part.astype(BF16)
+        to_peers(
+            chs * ys, ch * ys + own_y, xysend.at[n, order], xyrecv.at[n, order],
+            r_sem.at[n, 4 + 8 * order], r_sem.at[n, 5 + 8 * order], at_xy,
+        )
+        if order:
+            to_peers(ys, own_y, ygsend.at[n], ygrecv.at[n], r_sem.at[n, 6], r_sem.at[n, 7], at_y)
 
     def reduce_z_gates(n):
         arrived(ygrecv.at[n], r_sem.at[n, 7])
@@ -297,27 +317,37 @@
         zgsend[n] = total.astype(BF16)
         to_peers(zs, own_z, zgsend.at[n], zgrecv.at[n], r_sem.at[n, 8], r_sem.at[n, 9], at_z)
 
-    def reduce_z(n):
-        arrived(xyrecv.at[n], r_sem.at[n, 5])
-        total = xyrecv[n, 0].astype(F32)
+    def reduce_z(n, order):
+        arrived(xyrecv.at[n, order], r_sem.at[n, 5 + 8 * order])
+        total = xyrecv[n, order, 0].astype(F32)
         for a in range(1, chs * ys):
-            total = total + xyrecv[n, a].astype(F32)
-        total = total.reshape(2 * zs, grid)
+            total = total + xyrecv[n, order, a].astype(F32)
         for c in range(4):
-            thin[c] = total[:, c * LANES : (c + 1) * LANES]
-        for p in range(zs):
+            for b in range(2):
+                thin[c, b * 8 : b * 8 + zs // 2, :] = total[b, :, c * LANES : (c + 1) * LANES]
+        for p in range(zs // 2):
             for c in range(4):
-                zsend[n, p, :, c * LANES : (c + 1) * LANES] = thin[c, pl.ds(p, 2, stride=zs), :].astype(BF16)
-        to_peers(zs, own_z, zsend.at[n], zrecv.at[n], r_sem.at[n, 10], r_sem.at[n, 11], at_z)
+                to = 2 * p + class_of(order)
+                zsend[n, to, :, c * LANES : (c + 1) * LANES] = thin[c, pl.ds(p, 2, stride=8), :].astype(BF16)
+        for t in range(zs // 2):
+            d = (own_z + 2 * t + 1 - order) % zs
+            if order and t == 0:
+                pltpu.make_async_copy(zsend.at[n, own_z], zrecv.at[n, own_z], r_sem.at[n, 11]).start()
+            else:
+                pltpu.make_async_remote_copy(
+                    src_ref=zsend.at[n, d], dst_ref=zrecv.at[n, own_z],
+                    send_sem=r_sem.at[n, 10], recv_sem=r_sem.at[n, 11],
+                    device_id=at_z(d), device_id_type=MESH,
+                ).start()
 
     def finish(n, matrix_out, gates_out):
         arrived(zgrecv.at[n], r_sem.at[n, 9])
         gates_out[...] = jnp.sum(zgrecv[n].astype(F32), axis=0)
         arrived(zrecv.at[n], r_sem.at[n, 11])
         matrix_out[...] = jnp.sum(zrecv[n].astype(F32), axis=0)
-        for buffer, count, sem in (
-            (xysend, chs * ys, 4), (ygsend, ys, 6), (zgsend, zs, 8), (zsend, zs, 10)
-        ):
+        for order in range(2):
+            arrived(xysend.at[n, order, pl.ds(0, chs * ys - 1)], r_sem.at[n, 4 + 8 * order])
+        for buffer, count, sem in ((ygsend, ys, 6), (zgsend, zs, 8), (zsend, zs, 10)):
             arrived(buffer.at[n, pl.ds(0, count - 1)], r_sem.at[n, sem])
 
     def left_rows(p, q):
@@ -325,7 +355,7 @@
         return gl[r, :], gsecond[r, :]
 
     def right_rows_of(p, q):
-        r = pl.ds(pl.multiple_of(q * 8, 8), 8)
+        r = pl.ds(pl.multiple_of(q % 2 * part_rows + q // 2 * 8, 8), 8)
         return gr[p, r, :], gfirst[p, r, :]
 
     first_stage(0)
@@ -335,41 +365,56 @@
     spread(1)
     for load in loads[3:]:
         load.wait()
-    right_rows = right[...].astype(F32).reshape(pairs, 2, 8, grid)
+    right_rows = right[...].astype(F32).reshape(quads, 2, 2, 8, grid)
     for p in range(2):
-        right_t[p] = right_rows[:, p].reshape(grid // 2, grid).astype(BF16).T
+        both = jnp.concatenate([right_rows[:, zp, p].reshape(part_rows, grid) for zp in range(2)], axis=0)
+        right_t[p] = both.astype(BF16).T
 
     def split_gate(q, _):
-        rows = gate1[pl.ds(pl.multiple_of(q * 16, 16), 16), :].astype(F32)
-        for p in range(2):
-            gate1_p[p, pl.ds(pl.multiple_of(q * 8, 8), 8), :] = rows[p * 8 : p * 8 + 8]
+        rows = gate1[pl.ds(pl.multiple_of(q * 32, 32), 32), :].astype(F32)
+        for n in range(4):
+            to = pl.ds(pl.multiple_of(n // 2 * part_rows + q * 8, 8), 8)
+            gate1_p[n % 2, to, :] = rows[n * 8 : n * 8 + 8]
         return 0
 
-    lax.fori_loop(0, pairs, split_gate, 0)
+    lax.fori_loop(0, quads, split_gate, 0)
     gfirst[...] = jnp.zeros(gfirst.shape, F32)
     left_t[...] = left[...].T
     gl[...] = jnp.zeros(gl.shape, F32)
     gr[...] = jnp.zeros(gr.shape, F32)
     for h in range(2):
         middle(h)
-        send_back(h)
+        send_back(h, (0,) if h else (0, 1, 2))
         if h == 1:
             reduce_core(0, left_rows)
         write_out(h)
-    reduce_xy(0, left_rows)
-    last_stage(0, 0)
-    last_stage(0, 1)
+    core_arrived(0)
+    for order in range(2):
+        reduce_xy(0, left_rows, order)
+    rows_arrived(0, 0)
+    last_stage(0, 1 - core, 0, 2)
+    rows_arrived(0, 1)
+    rows_arrived(0, 2)
+    send_back(1, (1,))
+    last_stage(0, core, 0, 2)
     grad_of_inputs(0)
-    last_stage(1, 0)
+    rows_arrived(1, 0)
+    send_back(1, (2,))
+    last_stage(1, 1 - core, 0, 2)
     reduce_core(1, right_rows_of)
     reduce_z_gates(0)
-    reduce_z(0)
-    last_stage(1, 1)
-    reduce_xy(1, right_rows_of)
+    for order in range(2):
+        reduce_z(0, order)
+    core_arrived(1)
+    for order in range(2):
+        rows_arrived(1, order + 1)
+        last_stage(1, core, class_of(order), 1)
+        reduce_xy(1, right_rows_of, order)
+    reduce_z(1, 0)
     grad_of_inputs(1)
+    finish(0, gl_out, gs_out)
     reduce_z_gates(1)
-    reduce_z(1)
-    finish(0, gl_out, gs_out)
+    reduce_z(1, 1)
     finish(1, gr_out, gf_out)
     for h in range(2):
         arrived(fsend.at[h, pl.ds(0, seqs - 1)], fs_sem.at[h])
@@ -429,10 +474,10 @@
             v((grid, grid), F32), v((2, grid // 2, grid), F32), v((2, grid // 2, width), F32), v((grid, width), F32),
             v(block), v(block), v(block), v((2, 2, pairs, 8, 8, LANES)),
             *twice(pairs, 8, grid), *twice(pairs, 8, width),
-            v((4, pairs * 8, LANES), F32), *twice(chs * ys, 2, zs, grid),
+            v((4, pairs * 8, LANES), F32), *twice(2, chs * ys, 2, zs // 2, grid),
             *twice(ys, zs, 8, width),
             v((4, 2 * zs, LANES), F32), *twice(zs, 2, grid), *twice(zs, 8, width),
-            dma((6,)), dma((2,)), dma((2,)), dma((2,)), dma((2, 2)), dma((2, 12)),
+            dma((6,)), dma((2,)), dma((2,)), dma((2,)), dma((2, 3)), dma((2, 14)),
         ],
         compiler_params=pltpu.CompilerParams(
             collective_id=0, has_side_effects=True, vmem_limit_bytes=LIMIT_MIB * 1024 * 1024

time: 118 us -> 118 us (level)
  no operation moved by 1% of the time
where the time goes in v7:
time: 118 us; the launch traced here: 117 us
  Pallas kernels  117 us (99%)
    pallas_call x1, Pallas kernels, per_device(): pl.pallas_call(functools.partial(fused, seqs, zs, chs, grid), out_shape=s...  115 us

profile of v7, /device:TPU:24, one launch (start us, length us, event | category | flops | bytes accessed | tf_op | source)
XLA Modules:
  0.0 117.5 jit_solution(7410361086985988719)
XLA Ops:
  0.6 114.7 %shard_map.109 = (bf16[512,8,256]{2,1,0:T(8,128)(2,1)S(1)}, bf16[8,512,256]{2,1,0:T(8,128)(2,1)S(1)}, f32[2,512]{1,0:T(2,128)S(1)}, f32[2,512]{1,0:T(2,128)S(1)}...) custom-call(bf16[8,512,256]{2,1,0:T(8,128)(2,1)} %x_hbm.1, bf16[512,8,256]{2,1,0:T(8,128)(2,1)} %ct_hbm.1, ...), custom_call_target="tpu_custom_call" | custom-call | tf_op jit(solution)/shard_map/pallas_call | solution.py:465
  115.4 2.1 %shard_map.110 = (bf16[512,8,256]{2,1,0:T(8,128)(2,1)}, bf16[8,512,256]{2,1,0:T(8,128)(2,1)}, f32[2,512]{1,0:T(2,128)}, f32[2,512]{1,0:T(2,128)}, f32[8,256]{1,0:T(8,128)}, /*index=5*/f32[8,256]{1,0:T(8,128)}) custom-call(bf16[512,8,256]{2,1,0:T(8,128)(2,1)S(1)} %get-tuple-element.12.refs_0_, bf16[8,512,256]{2,1,0:T(8,128)(2,1)S(1)} %get-tuple-element.13.refs_1_, ...), custom_call_target="tpu_custom_call" | custom-call | tf_op jit(solution)/shard_map/pallas_call | solution.py:489
